TPU v7x, 32 devices: a whole 2x2x4 slice. The times are simulated.
32 devices in a mesh: row: 8 (over z, core), col: 4 (over y, x).
Axes of the slice: x: 2, y: 2, z: 4, core: 2. Of those that a mesh axis runs over, the one named last changes fastest.
Arguments:
- similarity: bfloat16 [2048, 2048], P('row', 'col')
- in_mask: int32 [8, 8], P('row', 'col'), may hold values from 0 to 1, as said below
- out_mask: int32 [8, 8], P('row', 'col'), may hold values from 0 to 1, as said below
Outputs:
- stochastic: float32 [2048, 2048], P('row', 'col')
Inputs may be any that keep to these rules, and one draw needn't show every extreme that they name: in_mask is symmetric, similarity is symmetric and nonnegative with positive diagonal entries, and every diagonal block is present. `out_mask`: every diagonal block is kept.
All inputs are finite; a program needn't handle non-finite values.
Results may differ from a plain program's by a relative error of at most 0.0003.
Values may be sent and summed in bfloat16 or wider, within the bound.
No kernel may reach another device: no remote copies, remote signals or barrier semaphores. Data moves between devices by JAX's collectives and lax.ppermute only.
A program may use at most 64 MiB of HBM per device.

v0:
```python
import jax
import jax.numpy as jnp
from jax import lax
from jax.sharding import PartitionSpec as P

BS = 256


def on_device(similarity, in_mask, out_mask):
    rows_loc, cols_loc = similarity.shape
    rblocks, cblocks = in_mask.shape
    live = in_mask.astype(jnp.bfloat16)[:, None, :, None]
    sparse = (similarity.reshape(rblocks, BS, cblocks, BS) * live).reshape(rows_loc, cols_loc)
    row_panel = lax.all_gather(sparse, "col", axis=1, tiled=True)
    product = jnp.dot(
        row_panel,
        lax.all_gather(sparse, "row", axis=0, tiled=True),
        preferred_element_type=jnp.float32,
    )
    keep = out_mask.astype(jnp.float32)[:, None, :, None]
    kept = (product.reshape(rblocks, BS, cblocks, BS) * keep).reshape(rows_loc, cols_loc)
    inflated = kept * kept
    column_sums = lax.psum(jnp.sum(inflated, axis=0), "row")
    total = jnp.float32(rows_loc * lax.axis_size("row"))
    return inflated * (total / column_sums)[None, :]


def solution(mesh):
    in_specs = (P("row", "col"), P("row", "col"), P("row", "col"))
    out_specs = P("row", "col")
    return jax.shard_map(
        on_device, mesh=mesh, in_specs=in_specs, out_specs=out_specs, check_vma=False
    )
```

profile of v0, /device:TPU:0, one launch (start us, length us, event | category | flops | bytes accessed | tf_op | source)
XLA Modules:
  0.0 94.9 jit_solution(12435030798267104924)
XLA Ops:
  6.5 0.0 all-gather.3.cloned.1.call-start
  6.5 0.7 convert_bitcast_fusion.1
  7.2 0.1 broadcast_bitcast_fusion.1
  7.3 1.7 %broadcast_multiply_fusion.1 = bf16[256,512]{1,0:T(8,128)(2,1)} fusion(bf16[256,512]{1,0:T(8,128)(2,1)} %param.3, bf16[512]{0:T(512)(128)(2,1)S(1)} %bitcast.12), kind=kLoop, calls=%fused_computation.3 | loop fusion | flops 131072 | bytes 525312 | tf_op jit(solution)/shard_map/mul | solution.py:13
  9.0 0.0 all-gather.3.cloned.1.call-update
  9.0 0.0 all-gather.5.cloned.1.call-start
  9.0 0.7 all-gather.5.cloned.1.call-update
  9.7 0.7 convert_bitcast_fusion
  10.4 0.1 broadcast_bitcast_fusion
  10.5 27.9 %all-gather.3.cloned.1.call-done = bf16[256,2048]{1,0:T(8,128)(2,1)} async-done(((bf16[256,512]{1,0:T(8,128)(2,1)}), bf16[256,2048]{1,0:T(8,128)(2,1)}) %all-gather.3.cloned.1.call-update) | async-done | bytes 1048592 | tf_op jit(solution)/shard_map/all_gather | solution.py:14
  38.4 30.7 %all-gather.5.cloned.1.call-done = bf16[2048,512]{1,0:T(8,128)(2,1)} async-done(((bf16[256,512]{1,0:T(8,128)(2,1)}), bf16[2048,512]{1,0:T(8,128)(2,1)}) %all-gather.5.cloned.1.call-update) | async-done | bytes 2097168 | tf_op jit(solution)/shard_map/all_gather | solution.py:17
  69.1 2.6 %fusion.1 = (f32[512]{0:T(512)S(1)}, f32[256,512]{1,0:T(8,128)S(1)}) fusion(f32[512]{0:T(512)S(1)} %bitcast.13, bf16[256,2048]{1,0:T(8,128)(2,1)} %all-gather.3.cloned.1.call-done, bf16[2048,512]{1,0:T(8,128)(2,1)} %all-gather.5.cloned.1.call-done), kind=kOutput, calls=%fused_computation.9 | convolution fusion | flops 537263616 | bytes 3674112 | tf_op jit(solution)/shard_map/dot_general | solution.py:15
  71.8 15.4 %psum.7 = f32[512]{0:T(512)S(1)} all-reduce(f32[512]{0:T(512)S(1)} %get-tuple-element.5), channel_id=1, replica_groups=mesh['row'=8,'col'=4] {'row'}, use_global_device_ids=true, to_apply=%region_1.0 | all-reduce | flops 512 | bytes 4096 | tf_op jit(solution)/shard_map/psum | solution.py:23
  87.2 0.9 broadcast_multiply_fusion
  (3 shorter events, 0.0 us)
Async XLA Ops:
  6.5 31.9 %all-gather.3.cloned.1.call-start = ((), (), s32[]{:S(2)}) async-start(), calls=%async_computation | async-start | bytes 1310720 | tf_op jit(solution)/shard_map/all_gather | solution.py:14
  9.0 60.2 %all-gather.5.cloned.1.call-start = ((), (), s32[]{:S(2)}) async-start(), calls=%async_computation.1 | async-start | bytes 2359296 | tf_op jit(solution)/shard_map/all_gather | solution.py:17
Sparse Core Ops, SparseCore 0:
  9.2 29.1 all-gather.2
  40.0 29.0 all-gather.4
where the time goes:
time: 95.1 us; the launch traced here: 94.9 us
  waiting for transfers between devices  59.4 us (62%)
  blocking collectives  15.4 us (16%)
  between operations  13.4 us (14%)
  other arithmetic  3.87 us (4%)
  matrix products  2.64 us (3%)
    all_gather x1, waiting for transfers between devices, on_device(): lax.all_gather(sparse, 'row', axis=0, tiled=True)  30.7 us
    all_gather x1, waiting for transfers between devices, on_device(): row_panel = lax.all_gather(sparse, 'col', axis=1, tiled=True)  27.9 us
    psum x1, blocking collectives, on_device(): column_sums = lax.psum(jnp.sum(inflated, axis=0), 'row')  15.4 us
    dot_general x1, matrix products, on_device(): jnp.dot(row_panel, lax.all_gather(sparse, 'row', axis=0, tiled=True), pre...  2.64 us
    mul x2, other arithmetic, on_device(): similarity.reshape(rblocks, BS, cblocks, BS) * live  2.33 us
  transfers between devices with their start and end apart: 2, of which 2 were waited for; matrix products, arithmetic and copies ran while one was open for 1% of the time, Pallas kernels for 0%

commit v1 on v0

v1 whole, which is shorter than its diff:
```python
import functools

import jax
import jax.numpy as jnp
from jax import lax
from jax.experimental import pallas as pl
from jax.experimental.pallas import tpu as pltpu
from jax.sharding import PartitionSpec as P

BS = 256


def swap(value, axis, size, mask):
    return lax.ppermute(value, axis, [(i, i ^ mask) for i in range(size)])


def early_kernel(n_col, n_z, last, place, *refs):
    panels = refs[:n_col]
    mine = refs[n_col : n_col + n_z - 1]
    theirs = refs[n_col + n_z - 1 : n_col + 2 * (n_z - 1)]
    acc_ref, late_ref, slots = refs[n_col + 2 * (n_z - 1) :]
    z, core, col = place[0], place[1], place[2]
    for j in range(n_col):
        slots[col ^ j] = panels[j][...]
    here = pl.ds(pl.multiple_of(core * BS, BS), BS)
    there = pl.ds(pl.multiple_of((1 - core) * BS, BS), BS)
    acc = None
    planes = [m for m in range(n_z) if m != last]
    for m, own, other in zip(planes, mine, theirs):
        panel = slots.at[z ^ m]
        term = jnp.dot(panel[:, here], own[...], preferred_element_type=jnp.float32)
        term += jnp.dot(panel[:, there], other[...], preferred_element_type=jnp.float32)
        acc = term if acc is None else acc + term
    acc_ref[...] = acc
    late_ref[...] = slots[z ^ last]


def late_kernel(place, keep, acc_ref, panel, own, other, out_ref, sums_ref):
    core = place[1]
    here = pl.ds(pl.multiple_of(core * BS, BS), BS)
    there = pl.ds(pl.multiple_of((1 - core) * BS, BS), BS)
    product = acc_ref[...]
    product += jnp.dot(panel[:, here], own[...], preferred_element_type=jnp.float32)
    product += jnp.dot(panel[:, there], other[...], preferred_element_type=jnp.float32)
    for b in range(product.shape[1] // BS):
        kept = jnp.where(keep[0, b] != 0, product[:, b * BS : (b + 1) * BS], 0.0)
        inflated = kept * kept
        out_ref[:, b * BS : (b + 1) * BS] = inflated
        sums_ref[:, b * BS : (b + 1) * BS] = jnp.sum(inflated, axis=0, keepdims=True)


def on_device(n_row, n_col, similarity, in_mask, out_mask):
    rows_loc, cols_loc = similarity.shape
    rblocks, cblocks = in_mask.shape
    n_z = n_row // 2
    live = in_mask.astype(jnp.bfloat16)[:, None, :, None]
    sparse = (similarity.reshape(rblocks, BS, cblocks, BS) * live).reshape(rows_loc, cols_loc)

    row = lax.axis_index("row")
    place = jnp.stack([row // 2, row % 2, lax.axis_index("col")]).astype(jnp.int32)

    mine = {m: swap(sparse, "row", n_row, 2 * m) for m in range(n_z - 1, 0, -1)}
    panels = [sparse] + [swap(sparse, "col", n_col, j) for j in range(1, n_col)]
    mine[0] = sparse
    theirs = {m: swap(mine[m], "row", n_row, 1) for m in range(n_z)}

    last = max(n_z // 2, 1)
    planes = [m for m in range(n_z) if m != last]
    smem = pl.BlockSpec(memory_space=pltpu.SMEM)
    vmem = pl.BlockSpec(memory_space=pltpu.VMEM)
    operands = panels + [mine[m] for m in planes] + [theirs[m] for m in planes]
    acc, late_panel = pl.pallas_call(
        functools.partial(early_kernel, n_col, n_z, last),
        out_shape=(
            jax.ShapeDtypeStruct((rows_loc, cols_loc), jnp.float32),
            jax.ShapeDtypeStruct((rows_loc, cols_loc), jnp.bfloat16),
        ),
        in_specs=[smem] + [vmem] * len(operands),
        out_specs=(vmem, vmem),
        scratch_shapes=[pltpu.VMEM((n_col, rows_loc, cols_loc), jnp.bfloat16)],
    )(place, *operands)
    inflated, sums = pl.pallas_call(
        late_kernel,
        out_shape=(
            jax.ShapeDtypeStruct((rows_loc, cols_loc), jnp.float32),
            jax.ShapeDtypeStruct((1, cols_loc), jnp.float32),
        ),
        in_specs=[smem, smem] + [vmem] * 4,
        out_specs=(vmem, vmem),
    )(place, out_mask, acc, late_panel, mine[last], theirs[last])

    step = 1
    while step < n_row:
        sums = sums + swap(sums, "row", n_row, step)
        step *= 2
    total = jnp.float32(rows_loc * n_row)
    return inflated * (total / sums)


def solution(mesh):
    in_specs = (P("row", "col"), P("row", "col"), P("row", "col"))
    out_specs = P("row", "col")
    body = functools.partial(on_device, mesh.shape["row"], mesh.shape["col"])
    return jax.shard_map(
        body, mesh=mesh, in_specs=in_specs, out_specs=out_specs, check_vma=False
    )
```

time: 95.1 us -> 51.2 us (0.54)
  waiting for transfers between devices: 59.4 us -> 24.8 us
  blocking collectives: 15.4 us -> 0 us
  between operations: 13.4 us -> 0.13 us
  starting transfers between devices: 0.04 us -> 13.3 us
  Pallas kernels: 0 us -> 5.47 us
  matrix products: 2.64 us -> 0 us
  local copies, waits for them, and re-layouts: 0.16 us -> 2.31 us
  other arithmetic: 3.87 us -> 4.86 us
    all_gather x2 -> x0, waiting for transfers between devices: 58.7 us -> none  [the longest x1 30.7 us: on_device(): lax.all_gather(sparse, 'row', axis=0, tiled=True)]
    ppermute x0 -> x13, waiting for transfers between devices: none -> 24.8 us  [swap(): return lax.ppermute(value, axis, [(i, i ^ mask) for i in range(size)])]
    psum x1 -> x0, blocking collectives: 15.4 us -> none  [on_device(): column_sums = lax.psum(jnp.sum(inflated, axis=0), 'row')]
    ppermute x0 -> x13, starting transfers between devices: none -> 13.3 us  [swap(): return lax.ppermute(value, axis, [(i, i ^ mask) for i in range(size)])]
    pallas_call x0 -> x2, Pallas kernels: none -> 5.47 us  [the longest x1 3.09 us: on_device(): pl.pallas_call(functools.partial(early_kernel, n_col, n_z, last), out_sha...]
    dot_general x1 -> x0, matrix products: 2.64 us -> none  [on_device(): jnp.dot(row_panel, lax.all_gather(sparse, 'row', axis=0, tiled=True), pre...]
    unnamed x4 -> x24, local copies, waits for them, and re-layouts: 0.16 us -> 2.31 us
    mul x2 -> x1, other arithmetic: 1.53 us -> 1.9 us  [on_device(): return inflated * (total / sums)]
  transfers between devices with their start and end apart: 2 -> 13, of which waited for: 2 -> 7; matrix products, arithmetic and copies ran while one was open for 1% -> 1% of each run, Pallas kernels for 0% -> 6%
where the time goes in v1:
time: 51.2 us; the launch traced here: 50.9 us
  waiting for transfers between devices  24.8 us (48%)
  starting transfers between devices  13.3 us (26%)
  Pallas kernels  5.47 us (11%)
  other arithmetic  4.86 us (9%)
  local copies, waits for them, and re-layouts  2.31 us (5%)
    ppermute x13, waiting for transfers between devices, swap(): return lax.ppermute(value, axis, [(i, i ^ mask) for i in range(size)])  24.8 us
    ppermute x13, starting transfers between devices, swap(): return lax.ppermute(value, axis, [(i, i ^ mask) for i in range(size)])  13.3 us
    pallas_call x1, Pallas kernels, on_device(): pl.pallas_call(functools.partial(early_kernel, n_col, n_z, last), out_sha...  3.09 us
    pallas_call x1, Pallas kernels, on_device(): pl.pallas_call(late_kernel, out_shape=(jax.ShapeDtypeStruct((rows_loc, co...  2.39 us
    unnamed x24, local copies, waits for them, and re-layouts  2.31 us
    mul x1, other arithmetic, on_device(): return inflated * (total / sums)  1.9 us
    mul x2, other arithmetic, on_device(): similarity.reshape(rblocks, BS, cblocks, BS) * live  1.63 us
  transfers between devices with their start and end apart: 13, of which 7 were waited for; matrix products, arithmetic and copies ran while one was open for 1% of the time, Pallas kernels for 6%

profile of v1, /device:TPU:0, one launch (start us, length us, event | category | flops | bytes accessed | tf_op | source)
XLA Modules:
  0.0 50.9 jit_solution(12935883462915128345)
XLA Ops:
  0.0 0.7 %convert_bitcast_fusion = bf16[2]{0:T(256)(128)(2,1)S(1)} fusion(s32[1,2]{1,0:T(1,128)} %param.4), kind=kLoop, calls=%fused_computation.4 | loop fusion | flops 2 | bytes 12 | tf_op jit(solution)/shard_map/mul | solution.py:57
  0.7 0.1 broadcast_bitcast_fusion
  0.7 1.0 %broadcast_multiply_fusion.1.refs_0_.refs_4_ = bf16[256,512]{1,0:T(8,128)(2,1)S(1)} fusion(bf16[256,512]{1,0:T(8,128)(2,1)} %param.3, bf16[512]{0:T(512)(128)(2,1)S(1)} %bitcast.10), kind=kLoop, calls=%fused_computation.1 | loop fusion | flops 131072 | bytes 525312 | tf_op jit(solution)/shard_map/mul | solution.py:57
  1.7 0.0 copy-start
  1.7 3.1 %collective-permute-start.3 = (bf16[256,512]{1,0:T(8,128)(2,1)S(1)}, bf16[256,512]{1,0:T(8,128)(2,1)S(1)}, u32[]{:S(2)}, u32[]{:S(2)}) collective-permute-start(bf16[256,512]{1,0:T(8,128)(2,1)S(1)} %broadcast_multiply_fusion.1.refs_0_.refs_4_), channel_id=1, source_target_pairs={{0,8},{4,12},{8,0},{12,4},{16,24},{20,28},{24,16},{28,20},{1,9},{5... | collective-permute-start | bytes 786440 | tf_op jit(solution)/shard_map/ppermute | solution.py:14
  4.8 2.5 %collective-permute-start.4 = (bf16[256,512]{1,0:T(8,128)(2,1)S(1)}, bf16[256,512]{1,0:T(8,128)(2,1)S(1)}, u32[]{:S(2)}, u32[]{:S(2)}) collective-permute-start(bf16[256,512]{1,0:T(8,128)(2,1)S(1)} %broadcast_multiply_fusion.1.refs_0_.refs_4_), channel_id=1, source_target_pairs={{0,24},{4,28},{8,16},{12,20},{16,8},{20,12},{24,0},{28,4},{1,25},{... | collective-permute-start | bytes 786440 | tf_op jit(solution)/shard_map/ppermute | solution.py:14
  7.3 1.5 %collective-permute-start = (bf16[256,512]{1,0:T(8,128)(2,1)S(1)}, bf16[256,512]{1,0:T(8,128)(2,1)S(1)}, u32[]{:S(2)}, u32[]{:S(2)}) collective-permute-start(bf16[256,512]{1,0:T(8,128)(2,1)S(1)} %broadcast_multiply_fusion.1.refs_0_.refs_4_), channel_id=1, source_target_pairs={{0,1},{1,0},{2,3},{3,2},{4,5},{5,4},{6,7},{7,6},{8,9},{9,8},{10,11... | collective-permute-start | bytes 786440 | tf_op jit(solution)/shard_map/ppermute | solution.py:14
  8.8 1.5 %collective-permute-start.1 = (bf16[256,512]{1,0:T(8,128)(2,1)S(1)}, bf16[256,512]{1,0:T(8,128)(2,1)S(1)}, u32[]{:S(2)}, u32[]{:S(2)}) collective-permute-start(bf16[256,512]{1,0:T(8,128)(2,1)S(1)} %broadcast_multiply_fusion.1.refs_0_.refs_4_), channel_id=1, source_target_pairs={{0,2},{1,3},{2,0},{3,1},{4,6},{5,7},{6,4},{7,5},{8,10},{9,11},{10,... | collective-permute-start | bytes 786440 | tf_op jit(solution)/shard_map/ppermute | solution.py:14
  10.3 0.1 collective-permute-start.8
  10.4 1.1 %collective-permute-done.3.refs_5_ = bf16[256,512]{1,0:T(8,128)(2,1)S(1)} collective-permute-done((bf16[256,512]{1,0:T(8,128)(2,1)S(1)}, bf16[256,512]{1,0:T(8,128)(2,1)S(1)}, u32[]{:S(2)}, u32[]{:S(2)}) %collective-permute-start.3) | collective-permute-done | bytes 262176 | tf_op jit(solution)/shard_map/ppermute | solution.py:14
  11.5 2.4 %collective-permute-start.2 = (bf16[256,512]{1,0:T(8,128)(2,1)S(1)}, bf16[256,512]{1,0:T(8,128)(2,1)S(1)}, u32[]{:S(2)}, u32[]{:S(2)}) collective-permute-start(bf16[256,512]{1,0:T(8,128)(2,1)S(1)} %broadcast_multiply_fusion.1.refs_0_.refs_4_), channel_id=1, source_target_pairs={{0,3},{1,2},{2,1},{3,0},{4,7},{5,6},{6,5},{7,4},{8,11},{9,10},{10,... | collective-permute-start | bytes 786440 | tf_op jit(solution)/shard_map/ppermute | solution.py:14
  14.0 6.2 %collective-permute-done.4.refs_6_ = bf16[256,512]{1,0:T(8,128)(2,1)S(1)} collective-permute-done((bf16[256,512]{1,0:T(8,128)(2,1)S(1)}, bf16[256,512]{1,0:T(8,128)(2,1)S(1)}, u32[]{:S(2)}, u32[]{:S(2)}) %collective-permute-start.4) | collective-permute-done | bytes 262176 | tf_op jit(solution)/shard_map/ppermute | solution.py:14
  20.2 0.0 collective-permute-start.5
  20.2 0.0 collective-permute-done.refs_1_
  20.2 0.0 copy-start.5
  20.2 0.5 collective-permute-start.6
  20.7 0.9 %collective-permute-done.1.refs_2_ = bf16[256,512]{1,0:T(8,128)(2,1)S(1)} collective-permute-done((bf16[256,512]{1,0:T(8,128)(2,1)S(1)}, bf16[256,512]{1,0:T(8,128)(2,1)S(1)}, u32[]{:S(2)}, u32[]{:S(2)}) %collective-permute-start.1) | collective-permute-done | bytes 262176 | tf_op jit(solution)/shard_map/ppermute | solution.py:14
  21.6 0.0 collective-permute-start.7
  21.6 8.7 %collective-permute-done.8.own = bf16[256,512]{1,0:T(8,128)(2,1)S(1)} collective-permute-done((bf16[256,512]{1,0:T(8,128)(2,1)S(1)}, bf16[256,512]{1,0:T(8,128)(2,1)S(1)}, u32[]{:S(2)}, u32[]{:S(2)}) %collective-permute-start.8) | collective-permute-done | bytes 262176 | tf_op jit(solution)/shard_map/ppermute | solution.py:14
  30.3 0.0 collective-permute-start.9
  30.3 0.6 %pad_add_fusion.place = s32[3]{0:T(128)} fusion(s32[1]{0:T(128)} %bitcast.2, s32[1]{0:T(128)} %bitcast.1, s32[1]{0:T(128)} %bitcast), kind=kLoop, calls=%fused_computation.3 | loop fusion | flops 6 | bytes 24 | tf_op jit(solution)/shard_map/stack | solution.py:60
  30.9 0.0 collective-permute-done.2.refs_3_
  30.9 0.0 collective-permute-done.5.refs_7_
  30.9 0.0 copy-start.8
  30.9 0.0 collective-permute-done.6.refs_8_
  31.0 0.0 copy-start.9
  31.0 0.0 collective-permute-done.7.refs_9_
  31.0 0.0 copy-done
  31.0 0.0 copy-done.3
  31.0 0.0 copy-done.4
  31.0 0.0 copy-done.5
  31.0 0.6 %copy-done.7 = bf16[256,512]{1,0:T(8,128)(2,1)} copy-done((bf16[256,512]{1,0:T(8,128)(2,1)}, bf16[256,512]{1,0:T(8,128)(2,1)S(1)}, u32[]{:S(2)}) %copy-start.7) | copy-done | bytes 262168
  31.6 0.1 copy-done.8
  31.7 0.1 copy-done.9
  31.8 0.7 %copy-done.10 = bf16[256,512]{1,0:T(8,128)(2,1)} copy-done((bf16[256,512]{1,0:T(8,128)(2,1)}, bf16[256,512]{1,0:T(8,128)(2,1)S(1)}, u32[]{:S(2)}) %copy-start.10) | copy-done | bytes 262168
  32.5 3.1 %shard_map.37 = (f32[256,512]{1,0:T(8,128)}, bf16[256,512]{1,0:T(8,128)(2,1)}) custom-call(s32[3]{0:T(128)} %pad_add_fusion.place, bf16[256,512]{1,0:T(8,128)(2,1)} %copy-done, bf16[256,512]{1,0:T(8,128)(2,1)} %copy-done.5, bf16[256,512]{1,0:T(8,128)(2,1)} %copy-done.6, bf16[256,512]{1,0:T(8,128)(2,1)} %copy-done.7, bf16[256,512]{1,0:T(8,128)(2,1)} %copy-done, ...), custom_call_target="tpu_custom_call" | custom-call | tf_op jit(solution)/shard_map/pallas_call | solution.py:72
  35.6 0.0 collective-permute-done.9.other
  35.6 0.0 copy-start.2
  35.6 0.7 %copy-done.2 = bf16[256,512]{1,0:T(8,128)(2,1)} copy-done((bf16[256,512]{1,0:T(8,128)(2,1)}, bf16[256,512]{1,0:T(8,128)(2,1)S(1)}, u32[]{:S(2)}) %copy-start.2) | copy-done | bytes 262168
  36.3 2.4 %shard_map.38 = (f32[256,512]{1,0:T(8,128)}, f32[1,512]{1,0:T(1,128)}) custom-call(s32[3]{0:T(128)} %pad_add_fusion.place, s32[1,2]{1,0:T(1,128)} %keep.1, f32[256,512]{1,0:T(8,128)} %get-tuple-element.9.acc_ref, bf16[256,512]{1,0:T(8,128)(2,1)} %get-tuple-element.10.panel, bf16[256,512]{1,0:T(8,128)(2,1)} %copy-done.1, bf16[256,512]{1,0:T(8,128)(2,1)} %copy-done.2), custom_call_target="tpu_custom_call" | custom-call | tf_op jit(solution)/shard_map/pallas_call | solution.py:82
  38.7 0.5 collective-permute-start.10
  39.2 1.0 %collective-permute-done.10 = f32[1,512]{1,0:T(1,128)S(1)} collective-permute-done((f32[1,512]{1,0:T(1,128)}, f32[1,512]{1,0:T(1,128)S(1)}, u32[]{:S(2)}, u32[]{:S(2)}) %collective-permute-start.10) | collective-permute-done | bytes 2080 | tf_op jit(solution)/shard_map/ppermute | solution.py:14
  40.3 0.7 %add.15 = f32[1,512]{1,0:T(1,128)S(1)} add(f32[1,512]{1,0:T(1,128)} %get-tuple-element.12, f32[1,512]{1,0:T(1,128)S(1)} %collective-permute-done.10) | non-fusion elementwise | flops 512 | bytes 6144 | tf_op jit(solution)/shard_map/add | solution.py:94
  40.9 0.0 collective-permute-start.11
  40.9 3.6 %collective-permute-done.11 = f32[1,512]{1,0:T(1,128)S(1)} collective-permute-done((f32[1,512]{1,0:T(1,128)S(1)}, f32[1,512]{1,0:T(1,128)S(1)}, u32[]{:S(2)}, u32[]{:S(2)}) %collective-permute-start.11) | collective-permute-done | bytes 2080 | tf_op jit(solution)/shard_map/ppermute | solution.py:14
  44.5 1.2 %collective-permute-start.12 = (f32[1,512]{1,0:T(1,128)S(1)}, f32[1,512]{1,0:T(1,128)S(1)}, u32[]{:S(2)}, u32[]{:S(2)}) collective-permute-start(f32[1,512]{1,0:T(1,128)S(1)} %add.16), channel_id=1, source_target_pairs={{0,16},{4,20},{8,24},{12,28},{16,0},{20,4},{24,8},{28,12},{1,17},{... | collective-permute-start | bytes 6152 | tf_op jit(solution)/shard_map/ppermute | solution.py:14
  45.7 3.3 %collective-permute-done.12 = f32[1,512]{1,0:T(1,128)S(1)} collective-permute-done((f32[1,512]{1,0:T(1,128)S(1)}, f32[1,512]{1,0:T(1,128)S(1)}, u32[]{:S(2)}, u32[]{:S(2)}) %collective-permute-start.12) | collective-permute-done | bytes 2080 | tf_op jit(solution)/shard_map/ppermute | solution.py:14
  49.0 1.9 %broadcast_multiply_fusion = f32[256,512]{1,0:T(8,128)} fusion(f32[256,512]{1,0:T(8,128)} %get-tuple-element.11, f32[512]{0:T(512)S(1)} %bitcast.9), kind=kLoop, calls=%fused_computation | loop fusion | flops 131072 | bytes 1050624 | tf_op jit(solution)/shard_map/mul | solution.py:97
  (11 shorter events, 0.0 us)
Async XLA Ops:
  1.7 29.3 %copy-start = (bf16[256,512]{1,0:T(8,128)(2,1)}, bf16[256,512]{1,0:T(8,128)(2,1)S(1)}, u32[]{:S(2)}) copy-start(bf16[256,512]{1,0:T(8,128)(2,1)S(1)} %broadcast_multiply_fusion.1.refs_0_.refs_4_) | copy-start | bytes 786436
  1.7 9.8 %collective-permute-start.3 = (bf16[256,512]{1,0:T(8,128)(2,1)S(1)}, bf16[256,512]{1,0:T(8,128)(2,1)S(1)}, u32[]{:S(2)}, u32[]{:S(2)}) collective-permute-start(bf16[256,512]{1,0:T(8,128)(2,1)S(1)} %broadcast_multiply_fusion.1.refs_0_.refs_4_), channel_id=1, source_target_pairs={{0,8},{4,12},{8,0},{12,4},{16,24},{20,28},{24,16},{28,20},{1,9},{5... | collective-permute-start | bytes 786440 | tf_op jit(solution)/shard_map/ppermute | solution.py:14
  4.8 15.4 %collective-permute-start.4 = (bf16[256,512]{1,0:T(8,128)(2,1)S(1)}, bf16[256,512]{1,0:T(8,128)(2,1)S(1)}, u32[]{:S(2)}, u32[]{:S(2)}) collective-permute-start(bf16[256,512]{1,0:T(8,128)(2,1)S(1)} %broadcast_multiply_fusion.1.refs_0_.refs_4_), channel_id=1, source_target_pairs={{0,24},{4,28},{8,16},{12,20},{16,8},{20,12},{24,0},{28,4},{1,25},{... | collective-permute-start | bytes 786440 | tf_op jit(solution)/shard_map/ppermute | solution.py:14
  7.3 12.9 %collective-permute-start = (bf16[256,512]{1,0:T(8,128)(2,1)S(1)}, bf16[256,512]{1,0:T(8,128)(2,1)S(1)}, u32[]{:S(2)}, u32[]{:S(2)}) collective-permute-start(bf16[256,512]{1,0:T(8,128)(2,1)S(1)} %broadcast_multiply_fusion.1.refs_0_.refs_4_), channel_id=1, source_target_pairs={{0,1},{1,0},{2,3},{3,2},{4,5},{5,4},{6,7},{7,6},{8,9},{9,8},{10,11... | collective-permute-start | bytes 786440 | tf_op jit(solution)/shard_map/ppermute | solution.py:14
  8.8 12.8 %collective-permute-start.1 = (bf16[256,512]{1,0:T(8,128)(2,1)S(1)}, bf16[256,512]{1,0:T(8,128)(2,1)S(1)}, u32[]{:S(2)}, u32[]{:S(2)}) collective-permute-start(bf16[256,512]{1,0:T(8,128)(2,1)S(1)} %broadcast_multiply_fusion.1.refs_0_.refs_4_), channel_id=1, source_target_pairs={{0,2},{1,3},{2,0},{3,1},{4,6},{5,7},{6,4},{7,5},{8,10},{9,11},{10,... | collective-permute-start | bytes 786440 | tf_op jit(solution)/shard_map/ppermute | solution.py:14
  10.3 20.0 %collective-permute-start.8 = (bf16[256,512]{1,0:T(8,128)(2,1)S(1)}, bf16[256,512]{1,0:T(8,128)(2,1)S(1)}, u32[]{:S(2)}, u32[]{:S(2)}) collective-permute-start(bf16[256,512]{1,0:T(8,128)(2,1)S(1)} %broadcast_multiply_fusion.1.refs_0_.refs_4_), channel_id=1, source_target_pairs={{0,16},{4,20},{8,24},{12,28},{16,0},{20,4},{24,8},{28,12},{1,17},{... | collective-permute-start | bytes 786440 | tf_op jit(solution)/shard_map/ppermute | solution.py:14
  11.5 19.5 %copy-start.3 = (bf16[256,512]{1,0:T(8,128)(2,1)}, bf16[256,512]{1,0:T(8,128)(2,1)S(1)}, u32[]{:S(2)}) copy-start(bf16[256,512]{1,0:T(8,128)(2,1)S(1)} %collective-permute-done.3.refs_5_) | copy-start | bytes 786436
  11.5 19.4 %collective-permute-start.2 = (bf16[256,512]{1,0:T(8,128)(2,1)S(1)}, bf16[256,512]{1,0:T(8,128)(2,1)S(1)}, u32[]{:S(2)}, u32[]{:S(2)}) collective-permute-start(bf16[256,512]{1,0:T(8,128)(2,1)S(1)} %broadcast_multiply_fusion.1.refs_0_.refs_4_), channel_id=1, source_target_pairs={{0,3},{1,2},{2,1},{3,0},{4,7},{5,6},{6,5},{7,4},{8,11},{9,10},{10,... | collective-permute-start | bytes 786440 | tf_op jit(solution)/shard_map/ppermute | solution.py:14
  20.2 10.8 %copy-start.4 = (bf16[256,512]{1,0:T(8,128)(2,1)}, bf16[256,512]{1,0:T(8,128)(2,1)S(1)}, u32[]{:S(2)}) copy-start(bf16[256,512]{1,0:T(8,128)(2,1)S(1)} %collective-permute-done.4.refs_6_) | copy-start | bytes 786436
  20.2 10.8 %collective-permute-start.5 = (bf16[256,512]{1,0:T(8,128)(2,1)S(1)}, bf16[256,512]{1,0:T(8,128)(2,1)S(1)}, u32[]{:S(2)}, u32[]{:S(2)}) collective-permute-start(bf16[256,512]{1,0:T(8,128)(2,1)S(1)} %broadcast_multiply_fusion.1.refs_0_.refs_4_), channel_id=1, source_target_pairs={{0,4},{4,0},{8,12},{12,8},{16,20},{20,16},{24,28},{28,24},{1,5},{5... | collective-permute-start | bytes 786440 | tf_op jit(solution)/shard_map/ppermute | solution.py:14
  20.2 10.8 %copy-start.5 = (bf16[256,512]{1,0:T(8,128)(2,1)}, bf16[256,512]{1,0:T(8,128)(2,1)S(1)}, u32[]{:S(2)}) copy-start(bf16[256,512]{1,0:T(8,128)(2,1)S(1)} %collective-permute-done.refs_1_) | copy-start | bytes 786436
  20.2 10.8 %collective-permute-start.6 = (bf16[256,512]{1,0:T(8,128)(2,1)S(1)}, bf16[256,512]{1,0:T(8,128)(2,1)S(1)}, u32[]{:S(2)}, u32[]{:S(2)}) collective-permute-start(bf16[256,512]{1,0:T(8,128)(2,1)S(1)} %collective-permute-done.3.refs_5_), channel_id=1, source_target_pairs={{0,4},{4,0},{8,12},{12,8},{16,20},{20,16},{24,28},{28,24},{1,5},{5... | collective-permute-start | bytes 786440 | tf_op jit(solution)/shard_map/ppermute | solution.py:14
  21.6 9.4 %copy-start.6 = (bf16[256,512]{1,0:T(8,128)(2,1)}, bf16[256,512]{1,0:T(8,128)(2,1)S(1)}, u32[]{:S(2)}) copy-start(bf16[256,512]{1,0:T(8,128)(2,1)S(1)} %collective-permute-done.1.refs_2_) | copy-start | bytes 786436
  21.6 9.4 %collective-permute-start.7 = (bf16[256,512]{1,0:T(8,128)(2,1)S(1)}, bf16[256,512]{1,0:T(8,128)(2,1)S(1)}, u32[]{:S(2)}, u32[]{:S(2)}) collective-permute-start(bf16[256,512]{1,0:T(8,128)(2,1)S(1)} %collective-permute-done.4.refs_6_), channel_id=1, source_target_pairs={{0,4},{4,0},{8,12},{12,8},{16,20},{20,16},{24,28},{28,24},{1,5},{5... | collective-permute-start | bytes 786440 | tf_op jit(solution)/shard_map/ppermute | solution.py:14
  30.3 5.3 %copy-start.1 = (bf16[256,512]{1,0:T(8,128)(2,1)}, bf16[256,512]{1,0:T(8,128)(2,1)S(1)}, u32[]{:S(2)}) copy-start(bf16[256,512]{1,0:T(8,128)(2,1)S(1)} %collective-permute-done.8.own) | copy-start | bytes 786436
  30.3 5.3 %collective-permute-start.9 = (bf16[256,512]{1,0:T(8,128)(2,1)S(1)}, bf16[256,512]{1,0:T(8,128)(2,1)S(1)}, u32[]{:S(2)}, u32[]{:S(2)}) collective-permute-start(bf16[256,512]{1,0:T(8,128)(2,1)S(1)} %collective-permute-done.8.own), channel_id=1, source_target_pairs={{0,4},{4,0},{8,12},{12,8},{16,20},{20,16},{24,28},{28,24},{1,5},{5... | collective-permute-start | bytes 786440 | tf_op jit(solution)/shard_map/ppermute | solution.py:14
  30.9 0.7 %copy-start.7 = (bf16[256,512]{1,0:T(8,128)(2,1)}, bf16[256,512]{1,0:T(8,128)(2,1)S(1)}, u32[]{:S(2)}) copy-start(bf16[256,512]{1,0:T(8,128)(2,1)S(1)} %collective-permute-done.2.refs_3_) | copy-start | bytes 786436
  30.9 0.8 %copy-start.8 = (bf16[256,512]{1,0:T(8,128)(2,1)}, bf16[256,512]{1,0:T(8,128)(2,1)S(1)}, u32[]{:S(2)}) copy-start(bf16[256,512]{1,0:T(8,128)(2,1)S(1)} %collective-permute-done.5.refs_7_) | copy-start | bytes 786436
  31.0 0.9 %copy-start.9 = (bf16[256,512]{1,0:T(8,128)(2,1)}, bf16[256,512]{1,0:T(8,128)(2,1)S(1)}, u32[]{:S(2)}) copy-start(bf16[256,512]{1,0:T(8,128)(2,1)S(1)} %collective-permute-done.6.refs_8_) | copy-start | bytes 786436
  31.8 0.7 %copy-start.10 = (bf16[256,512]{1,0:T(8,128)(2,1)}, bf16[256,512]{1,0:T(8,128)(2,1)S(1)}, u32[]{:S(2)}) copy-start(bf16[256,512]{1,0:T(8,128)(2,1)S(1)} %collective-permute-done.7.refs_9_) | copy-start | bytes 786436
  35.6 0.7 %copy-start.2 = (bf16[256,512]{1,0:T(8,128)(2,1)}, bf16[256,512]{1,0:T(8,128)(2,1)S(1)}, u32[]{:S(2)}) copy-start(bf16[256,512]{1,0:T(8,128)(2,1)S(1)} %collective-permute-done.9.other) | copy-start | bytes 786436
  38.7 1.5 %collective-permute-start.10 = (f32[1,512]{1,0:T(1,128)}, f32[1,512]{1,0:T(1,128)S(1)}, u32[]{:S(2)}, u32[]{:S(2)}) collective-permute-start(f32[1,512]{1,0:T(1,128)} %get-tuple-element.12), channel_id=1, source_target_pairs={{0,4},{4,0},{8,12},{12,8},{16,20},{20,16},{24,28},{28,24},{1,5},{5... | collective-permute-start | bytes 6152 | tf_op jit(solution)/shard_map/ppermute | solution.py:14
  40.9 3.6 %collective-permute-start.11 = (f32[1,512]{1,0:T(1,128)S(1)}, f32[1,512]{1,0:T(1,128)S(1)}, u32[]{:S(2)}, u32[]{:S(2)}) collective-permute-start(f32[1,512]{1,0:T(1,128)S(1)} %add.15), channel_id=1, source_target_pairs={{0,8},{4,12},{8,0},{12,4},{16,24},{20,28},{24,16},{28,20},{1,9},{5... | collective-permute-start | bytes 6152 | tf_op jit(solution)/shard_map/ppermute | solution.py:14
  44.5 4.5 %collective-permute-start.12 = (f32[1,512]{1,0:T(1,128)S(1)}, f32[1,512]{1,0:T(1,128)S(1)}, u32[]{:S(2)}, u32[]{:S(2)}) collective-permute-start(f32[1,512]{1,0:T(1,128)S(1)} %add.16), channel_id=1, source_target_pairs={{0,16},{4,20},{8,24},{12,28},{16,0},{20,4},{24,8},{28,12},{1,17},{... | collective-permute-start | bytes 6152 | tf_op jit(solution)/shard_map/ppermute | solution.py:14

commit v2 on v1

v2 whole, which is shorter than its diff:
```python
import functools

import jax
import jax.numpy as jnp
from jax import lax
from jax.experimental import pallas as pl
from jax.experimental.pallas import tpu as pltpu
from jax.sharding import PartitionSpec as P

BS = 256


def swap(value, axis, size, mask):
    return lax.ppermute(value, axis, [(i, i ^ mask) for i in range(size)])


def along_z(value, pairs):
    return lax.ppermute(value, "row", [(2 * s + k, 2 * t + k) for s, t in pairs for k in (0, 1)])


def resident(value):
    return pltpu.with_memory_space_constraint(value, pltpu.VMEM)


def term(panel, core, own, other):
    here = pl.ds(pl.multiple_of(core * BS, BS), BS)
    there = pl.ds(pl.multiple_of((1 - core) * BS, BS), BS)
    return jnp.dot(
        panel[:, here], own[...], preferred_element_type=jnp.float32
    ) + jnp.dot(panel[:, there], other[...], preferred_element_type=jnp.float32)


def early_kernel(n_col, planes, last, place, *refs):
    panels = refs[:n_col]
    mine = refs[n_col : n_col + len(planes)]
    theirs = refs[n_col + len(planes) : n_col + 2 * len(planes)]
    acc_ref, late_ref, slots = refs[n_col + 2 * len(planes) :]
    z, core, col = place[0], place[1], place[2]
    for j in range(n_col):
        slots[col ^ j] = panels[j][...]
    acc = None
    for m, own, other in zip(planes, mine, theirs):
        part = term(slots.at[z ^ m], core, own, other)
        acc = part if acc is None else acc + part
    acc_ref[...] = acc
    late_ref[...] = slots[z ^ last]


def late_kernel(place, keep, acc_ref, panel, own, other, out_ref, sums_ref):
    product = acc_ref[...] + term(panel, place[1], own, other)
    for b in range(product.shape[1] // BS):
        kept = jnp.where(keep[0, b] != 0, product[:, b * BS : (b + 1) * BS], 0.0)
        inflated = kept * kept
        out_ref[:, b * BS : (b + 1) * BS] = inflated
        sums_ref[:, b * BS : (b + 1) * BS] = jnp.sum(inflated, axis=0, keepdims=True)


def gather(sparse, n_row, n_col):
    n_z = n_row // 2
    ends = n_z == 4
    panels = {1 << i: swap(sparse, "col", n_col, 1 << i) for i in range(n_col.bit_length() - 1)}
    if ends:
        blocks = {m: along_z(sparse, [(i, i ^ m) for i in range(4)]) for m in (1, 2)}
    else:
        blocks = {m: swap(sparse, "row", n_row, 2 * m) for m in range(1, n_z)}
    other = swap(sparse, "row", n_row, 1)
    names = [(blocks, m) for m in sorted(blocks, reverse=True)]
    names += [(panels, j) for j in sorted(panels)]
    *moved, other, source = lax.optimization_barrier([d[k] for d, k in names] + [other, sparse])
    for (d, k), value in zip(names, moved):
        d[k] = value
    if ends:
        middle = along_z(source, [(1, 2), (2, 1)])
        pairs = [(1, blocks[1]), (2, blocks[2]), (3, middle)]
        pairs.append((3, along_z(blocks[2], [(1, 0), (2, 3)])))
    else:
        pairs = list(blocks.items())
    panels[0] = sparse
    for j in range(n_col):
        if j not in panels:
            low = j & -j
            panels[j] = swap(panels[j ^ low], "col", n_col, low)
    theirs = [other] + [swap(block, "row", n_row, 1) for _, block in pairs]
    return [panels[j] for j in range(n_col)], [(0, sparse)] + pairs, theirs


def on_device(n_row, n_col, similarity, in_mask, out_mask):
    rows_loc, cols_loc = similarity.shape
    rblocks, cblocks = in_mask.shape
    live = in_mask.astype(jnp.bfloat16)[:, None, :, None]
    sparse = (similarity.reshape(rblocks, BS, cblocks, BS) * live).reshape(rows_loc, cols_loc)

    row = lax.axis_index("row")
    place = jnp.stack([row // 2, row % 2, lax.axis_index("col")]).astype(jnp.int32)
    panels, mine, theirs = gather(sparse, n_row, n_col)
    last, late = mine.pop()
    other = theirs.pop()

    smem = pl.BlockSpec(memory_space=pltpu.SMEM)
    vmem = pl.BlockSpec(memory_space=pltpu.VMEM)
    size = 2 * rows_loc * cols_loc
    operands = panels + [block for _, block in mine] + theirs
    acc, late_panel = pl.pallas_call(
        functools.partial(early_kernel, n_col, [m for m, _ in mine], last),
        out_shape=(
            pltpu.VMEM((rows_loc, cols_loc), jnp.float32),
            pltpu.VMEM((rows_loc, cols_loc), jnp.bfloat16),
        ),
        in_specs=[smem] + [vmem] * len(operands),
        out_specs=(vmem, vmem),
        scratch_shapes=[pltpu.VMEM((n_col, rows_loc, cols_loc), jnp.bfloat16)],
        compiler_params=pltpu.CompilerParams(vmem_limit_bytes=(n_col + 8) * size),
    )(place, *map(resident, operands))
    inflated, sums = pl.pallas_call(
        late_kernel,
        out_shape=(
            pltpu.VMEM((rows_loc, cols_loc), jnp.float32),
            pltpu.VMEM((1, cols_loc), jnp.float32),
        ),
        in_specs=[smem, smem] + [vmem] * 4,
        out_specs=(vmem, vmem),
        compiler_params=pltpu.CompilerParams(vmem_limit_bytes=8 * size),
    )(place, out_mask, acc, late_panel, resident(late), resident(other))

    step = 1
    while step < n_row:
        sums = sums + swap(sums, "row", n_row, step)
        step *= 2
    total = jnp.float32(rows_loc * n_row)
    return inflated * (total / sums)


def solution(mesh):
    in_specs = (P("row", "col"), P("row", "col"), P("row", "col"))
    out_specs = P("row", "col")
    body = functools.partial(on_device, mesh.shape["row"], mesh.shape["col"])
    return jax.shard_map(
        body, mesh=mesh, in_specs=in_specs, out_specs=out_specs, check_vma=False
    )
```

time: 51.2 us -> 43.6 us (0.85)
  waiting for transfers between devices: 24.8 us -> 18.3 us
  starting transfers between devices: 13.3 us -> 19.5 us
  Pallas kernels: 5.47 us -> 2.15 us
  other arithmetic: 4.86 us -> 2.58 us
  local copies, waits for them, and re-layouts: 2.31 us -> 0.73 us
    ppermute x13 -> x11, waiting for transfers between devices: 24.8 us -> 4.54 us  [swap(): return lax.ppermute(value, axis, [(i, i ^ mask) for i in range(size)])]
    ppermute x0 -> x4, waiting for transfers between devices: none -> 13.8 us  [along_z(): lax.ppermute(value, 'row', [(2 * s + k, 2 * t + k) for s, t in pairs for...]
    ppermute x0 -> x4, starting transfers between devices: none -> 7.65 us  [along_z(): lax.ppermute(value, 'row', [(2 * s + k, 2 * t + k) for s, t in pairs for...]
    pallas_call x2, Pallas kernels: 5.47 us -> 2.15 us  [the longest x1 1.3 us: on_device(): pl.pallas_call(functools.partial(early_kernel, n_col, [m for m, _ in mine...]
    unnamed x24 -> x4, local copies, waits for them, and re-layouts: 2.31 us -> 0.73 us
    ppermute x13 -> x11, starting transfers between devices: 13.3 us -> 11.9 us  [swap(): return lax.ppermute(value, axis, [(i, i ^ mask) for i in range(size)])]
    mul x1, other arithmetic: 1.9 us -> 0.86 us  [on_device(): return inflated * (total / sums)]
    add x2, other arithmetic: 0.68 us -> 0.01 us  [on_device(): sums = sums + swap(sums, 'row', n_row, step)]
  transfers between devices with their start and end apart: 13 -> 15, of which waited for: 7 -> 7; matrix products, arithmetic and copies ran while one was open for 1% -> 0% of each run, Pallas kernels for 6% -> 3%
where the time goes in v2:
time: 43.6 us; the launch traced here: 43.4 us
  starting transfers between devices  19.5 us (45%)
  waiting for transfers between devices  18.3 us (42%)
  other arithmetic  2.58 us (6%)
  Pallas kernels  2.15 us (5%)
  local copies, waits for them, and re-layouts  0.73 us (2%)
    ppermute x4, waiting for transfers between devices, along_z(): lax.ppermute(value, 'row', [(2 * s + k, 2 * t + k) for s, t in pairs for...  13.8 us
    ppermute x11, starting transfers between devices, swap(): return lax.ppermute(value, axis, [(i, i ^ mask) for i in range(size)])  11.9 us
    ppermute x4, starting transfers between devices, along_z(): lax.ppermute(value, 'row', [(2 * s + k, 2 * t + k) for s, t in pairs for...  7.65 us
    ppermute x11, waiting for transfers between devices, swap(): return lax.ppermute(value, axis, [(i, i ^ mask) for i in range(size)])  4.54 us
    mul x2, other arithmetic, on_device(): similarity.reshape(rblocks, BS, cblocks, BS) * live  1.63 us
    pallas_call x1, Pallas kernels, on_device(): pl.pallas_call(functools.partial(early_kernel, n_col, [m for m, _ in mine...  1.3 us
  transfers between devices with their start and end apart: 15, of which 7 were waited for; matrix products, arithmetic and copies ran while one was open for 0% of the time, Pallas kernels for 3%

profile of v2, /device:TPU:0, one launch (start us, length us, event | category | flops | bytes accessed | tf_op | source)
XLA Modules:
  0.0 43.4 jit_solution(15283100759099429384)
XLA Ops:
  0.0 0.7 %convert_bitcast_fusion = bf16[2]{0:T(256)(128)(2,1)S(1)} fusion(s32[1,2]{1,0:T(1,128)} %param.4), kind=kLoop, calls=%fused_computation.4 | loop fusion | flops 2 | bytes 12 | tf_op jit(solution)/shard_map/mul | solution.py:91
  0.7 0.1 broadcast_bitcast_fusion
  0.7 1.0 %broadcast_multiply_fusion.1.refs_0_.refs_4_ = bf16[256,512]{1,0:T(8,128)(2,1)S(1)} fusion(bf16[256,512]{1,0:T(8,128)(2,1)} %param.3, bf16[512]{0:T(512)(128)(2,1)S(1)} %bitcast.10), kind=kLoop, calls=%fused_computation.1 | loop fusion | flops 131072 | bytes 525312 | tf_op jit(solution)/shard_map/mul | solution.py:91
  1.7 4.1 %collective-permute-start = (bf16[256,512]{1,0:T(8,128)(2,1)S(1)}, bf16[256,512]{1,0:T(8,128)(2,1)S(1)}, u32[]{:S(2)}, u32[]{:S(2)}) collective-permute-start(bf16[256,512]{1,0:T(8,128)(2,1)S(1)} %broadcast_multiply_fusion.1.refs_0_.refs_4_), channel_id=1, source_target_pairs={{0,16},{4,20},{8,24},{12,28},{16,0},{20,4},{24,8},{28,12},{1,17},{... | collective-permute-start | bytes 786440 | tf_op jit(solution)/shard_map/ppermute | solution.py:18
  5.8 1.6 %collective-permute-start.1 = (bf16[256,512]{1,0:T(8,128)(2,1)S(1)}, bf16[256,512]{1,0:T(8,128)(2,1)S(1)}, u32[]{:S(2)}, u32[]{:S(2)}) collective-permute-start(bf16[256,512]{1,0:T(8,128)(2,1)S(1)} %broadcast_multiply_fusion.1.refs_0_.refs_4_), channel_id=1, source_target_pairs={{0,8},{4,12},{8,0},{12,4},{16,24},{20,28},{24,16},{28,20},{1,9},{5... | collective-permute-start | bytes 786440 | tf_op jit(solution)/shard_map/ppermute | solution.py:18
  7.4 1.5 %collective-permute-start.2 = (bf16[256,512]{1,0:T(8,128)(2,1)S(1)}, bf16[256,512]{1,0:T(8,128)(2,1)S(1)}, u32[]{:S(2)}, u32[]{:S(2)}) collective-permute-start(bf16[256,512]{1,0:T(8,128)(2,1)S(1)} %broadcast_multiply_fusion.1.refs_0_.refs_4_), channel_id=1, source_target_pairs={{0,1},{1,0},{2,3},{3,2},{4,5},{5,4},{6,7},{7,6},{8,9},{9,8},{10,11... | collective-permute-start | bytes 786440 | tf_op jit(solution)/shard_map/ppermute | solution.py:14
  8.9 1.5 %collective-permute-start.3 = (bf16[256,512]{1,0:T(8,128)(2,1)S(1)}, bf16[256,512]{1,0:T(8,128)(2,1)S(1)}, u32[]{:S(2)}, u32[]{:S(2)}) collective-permute-start(bf16[256,512]{1,0:T(8,128)(2,1)S(1)} %broadcast_multiply_fusion.1.refs_0_.refs_4_), channel_id=1, source_target_pairs={{0,2},{1,3},{2,0},{3,1},{4,6},{5,7},{6,4},{7,5},{8,10},{9,11},{10,... | collective-permute-start | bytes 786440 | tf_op jit(solution)/shard_map/ppermute | solution.py:14
  10.4 0.0 collective-permute-start.4
  10.4 7.4 %collective-permute-done.refs_6_ = bf16[256,512]{1,0:T(8,128)(2,1)S(1)} collective-permute-done((bf16[256,512]{1,0:T(8,128)(2,1)S(1)}, bf16[256,512]{1,0:T(8,128)(2,1)S(1)}, u32[]{:S(2)}, u32[]{:S(2)}) %collective-permute-start) | collective-permute-done | bytes 262176 | tf_op jit(solution)/shard_map/ppermute | solution.py:18
  17.8 0.2 collective-permute-done.1.refs_5_
  18.0 0.0 collective-permute-done.2.refs_1_
  18.0 0.0 collective-permute-done.3.refs_2_
  18.0 0.0 collective-permute-done.4.refs_8_
  18.1 0.7 %collective-permute-start.6 = (bf16[256,512]{1,0:T(8,128)(2,1)S(1)}, bf16[256,512]{1,0:T(8,128)(2,1)S(1)}, u32[]{:S(2)}, u32[]{:S(2)}) collective-permute-start(bf16[256,512]{1,0:T(8,128)(2,1)S(1)} %broadcast_multiply_fusion.1.refs_0_.refs_4_), channel_id=1, source_target_pairs={{8,16},{12,20},{16,8},{20,12},{9,17},{13,21},{17,9},{21,13},{10,18... | collective-permute-start | bytes 786440 | tf_op jit(solution)/shard_map/ppermute | solution.py:18
  18.7 1.3 %collective-permute-start.10 = (bf16[256,512]{1,0:T(8,128)(2,1)S(1)}, bf16[256,512]{1,0:T(8,128)(2,1)S(1)}, u32[]{:S(2)}, u32[]{:S(2)}) collective-permute-start(bf16[256,512]{1,0:T(8,128)(2,1)S(1)} %collective-permute-done.refs_6_), channel_id=1, source_target_pairs={{8,0},{12,4},{16,24},{20,28},{9,1},{13,5},{17,25},{21,29},{10,2},{... | collective-permute-start | bytes 786440 | tf_op jit(solution)/shard_map/ppermute | solution.py:18
  20.0 0.1 collective-permute-start.8
  20.1 1.6 %collective-permute-start.5 = (bf16[256,512]{1,0:T(8,128)(2,1)S(1)}, bf16[256,512]{1,0:T(8,128)(2,1)S(1)}, u32[]{:S(2)}, u32[]{:S(2)}) collective-permute-start(bf16[256,512]{1,0:T(8,128)(2,1)S(1)} %collective-permute-done.3.refs_2_), channel_id=1, source_target_pairs={{0,1},{1,0},{2,3},{3,2},{4,5},{5,4},{6,7},{7,6},{8,9},{9,8},{10,11... | collective-permute-start | bytes 786440 | tf_op jit(solution)/shard_map/ppermute | solution.py:14
  21.7 0.2 collective-permute-start.7
  21.9 0.0 collective-permute-done.6.refs_7_
  21.9 0.3 collective-permute-start.9
  22.2 6.1 %collective-permute-done.10.own = bf16[256,512]{1,0:T(8,128)(2,1)S(1)} collective-permute-done((bf16[256,512]{1,0:T(8,128)(2,1)S(1)}, bf16[256,512]{1,0:T(8,128)(2,1)S(1)}, u32[]{:S(2)}, u32[]{:S(2)}) %collective-permute-start.10) | collective-permute-done | bytes 262176 | tf_op jit(solution)/shard_map/ppermute | solution.py:18
  28.4 0.0 collective-permute-start.11
  28.4 0.1 pad_add_fusion.place
  28.5 0.0 collective-permute-done.8.refs_10_
  28.5 0.4 collective-permute-done.5.refs_3_
  28.8 0.0 collective-permute-done.7.refs_9_
  28.8 0.0 collective-permute-done.9.refs_11_
  28.8 1.3 %shard_map.37 = (f32[256,512]{1,0:T(8,128)S(1)}, bf16[256,512]{1,0:T(8,128)(2,1)S(1)}) custom-call(s32[3]{0:T(128)S(1)} %pad_add_fusion.place, bf16[256,512]{1,0:T(8,128)(2,1)S(1)} %broadcast_multiply_fusion.1.refs_0_.refs_4_, bf16[256,512]{1,0:T(8,128)(2,1)S(1)} %collective-permute-done.2.refs_1_, bf16[256,512]{1,0:T(8,128)(2,1)S(1)} %collective-permute-done.3.refs_2_, ...), custom_call_target="tpu_custom_call" | custom-call | tf_op jit(solution)/shard_map/pallas_call | solution.py:103
  30.1 0.0 collective-permute-done.11.other
  30.2 0.0 copy-start
  30.2 0.6 %copy-done = s32[1,2]{1,0:T(1,128)S(1)} copy-done((s32[1,2]{1,0:T(1,128)S(1)}, s32[1,2]{1,0:T(1,128)}, u32[]{:S(2)}) %copy-start) | copy-done | bytes 32
  30.8 0.9 %shard_map.38 = (f32[256,512]{1,0:T(8,128)S(1)}, f32[1,512]{1,0:T(1,128)S(1)}) custom-call(s32[3]{0:T(128)S(1)} %pad_add_fusion.place, s32[1,2]{1,0:T(1,128)S(1)} %copy-done, f32[256,512]{1,0:T(8,128)S(1)} %get-tuple-element.21.acc_ref, bf16[256,512]{1,0:T(8,128)(2,1)S(1)} %get-tuple-element.22.panel, bf16[256,512]{1,0:T(8,128)(2,1)S(1)} %collective-permute-done.10.own, ...), custom_call_target="tpu_custom_call" | custom-call | tf_op jit(solution)/shard_map/pallas_call | solution.py:114
  31.7 0.2 collective-permute-start.12
  31.9 1.0 %collective-permute-done.12 = f32[1,512]{1,0:T(1,128)S(1)} collective-permute-done((f32[1,512]{1,0:T(1,128)S(1)}, f32[1,512]{1,0:T(1,128)S(1)}, u32[]{:S(2)}, u32[]{:S(2)}) %collective-permute-start.12) | collective-permute-done | bytes 2080 | tf_op jit(solution)/shard_map/ppermute | solution.py:14
  32.9 3.2 %collective-permute-start.13 = (f32[1,512]{1,0:T(1,128)S(1)}, f32[1,512]{1,0:T(1,128)S(1)}, u32[]{:S(2)}, u32[]{:S(2)}) collective-permute-start(f32[1,512]{1,0:T(1,128)S(1)} %add.15), channel_id=1, source_target_pairs={{0,8},{4,12},{8,0},{12,4},{16,24},{20,28},{24,16},{28,20},{1,9},{5... | collective-permute-start | bytes 6152 | tf_op jit(solution)/shard_map/ppermute | solution.py:14
  36.1 1.6 %collective-permute-done.13 = f32[1,512]{1,0:T(1,128)S(1)} collective-permute-done((f32[1,512]{1,0:T(1,128)S(1)}, f32[1,512]{1,0:T(1,128)S(1)}, u32[]{:S(2)}, u32[]{:S(2)}) %collective-permute-start.13) | collective-permute-done | bytes 2080 | tf_op jit(solution)/shard_map/ppermute | solution.py:14
  37.7 3.3 %collective-permute-start.14 = (f32[1,512]{1,0:T(1,128)S(1)}, f32[1,512]{1,0:T(1,128)S(1)}, u32[]{:S(2)}, u32[]{:S(2)}) collective-permute-start(f32[1,512]{1,0:T(1,128)S(1)} %add.16), channel_id=1, source_target_pairs={{0,16},{4,20},{8,24},{12,28},{16,0},{20,4},{24,8},{28,12},{1,17},{... | collective-permute-start | bytes 6152 | tf_op jit(solution)/shard_map/ppermute | solution.py:14
  40.9 1.6 %collective-permute-done.14 = f32[1,512]{1,0:T(1,128)S(1)} collective-permute-done((f32[1,512]{1,0:T(1,128)S(1)}, f32[1,512]{1,0:T(1,128)S(1)}, u32[]{:S(2)}, u32[]{:S(2)}) %collective-permute-start.14) | collective-permute-done | bytes 2080 | tf_op jit(solution)/shard_map/ppermute | solution.py:14
  42.5 0.9 %broadcast_multiply_fusion = f32[256,512]{1,0:T(8,128)} fusion(f32[256,512]{1,0:T(8,128)S(1)} %get-tuple-element.23, f32[512]{0:T(512)S(1)} %bitcast.9), kind=kLoop, calls=%fused_computation | loop fusion | flops 131072 | bytes 1050624 | tf_op jit(solution)/shard_map/mul | solution.py:130
  (4 shorter events, 0.0 us)
Async XLA Ops:
  1.7 16.1 %collective-permute-start = (bf16[256,512]{1,0:T(8,128)(2,1)S(1)}, bf16[256,512]{1,0:T(8,128)(2,1)S(1)}, u32[]{:S(2)}, u32[]{:S(2)}) collective-permute-start(bf16[256,512]{1,0:T(8,128)(2,1)S(1)} %broadcast_multiply_fusion.1.refs_0_.refs_4_), channel_id=1, source_target_pairs={{0,16},{4,20},{8,24},{12,28},{16,0},{20,4},{24,8},{28,12},{1,17},{... | collective-permute-start | bytes 786440 | tf_op jit(solution)/shard_map/ppermute | solution.py:18
  5.8 12.2 %collective-permute-start.1 = (bf16[256,512]{1,0:T(8,128)(2,1)S(1)}, bf16[256,512]{1,0:T(8,128)(2,1)S(1)}, u32[]{:S(2)}, u32[]{:S(2)}) collective-permute-start(bf16[256,512]{1,0:T(8,128)(2,1)S(1)} %broadcast_multiply_fusion.1.refs_0_.refs_4_), channel_id=1, source_target_pairs={{0,8},{4,12},{8,0},{12,4},{16,24},{20,28},{24,16},{28,20},{1,9},{5... | collective-permute-start | bytes 786440 | tf_op jit(solution)/shard_map/ppermute | solution.py:18
  7.4 10.6 %collective-permute-start.2 = (bf16[256,512]{1,0:T(8,128)(2,1)S(1)}, bf16[256,512]{1,0:T(8,128)(2,1)S(1)}, u32[]{:S(2)}, u32[]{:S(2)}) collective-permute-start(bf16[256,512]{1,0:T(8,128)(2,1)S(1)} %broadcast_multiply_fusion.1.refs_0_.refs_4_), channel_id=1, source_target_pairs={{0,1},{1,0},{2,3},{3,2},{4,5},{5,4},{6,7},{7,6},{8,9},{9,8},{10,11... | collective-permute-start | bytes 786440 | tf_op jit(solution)/shard_map/ppermute | solution.py:14
  8.9 9.2 %collective-permute-start.3 = (bf16[256,512]{1,0:T(8,128)(2,1)S(1)}, bf16[256,512]{1,0:T(8,128)(2,1)S(1)}, u32[]{:S(2)}, u32[]{:S(2)}) collective-permute-start(bf16[256,512]{1,0:T(8,128)(2,1)S(1)} %broadcast_multiply_fusion.1.refs_0_.refs_4_), channel_id=1, source_target_pairs={{0,2},{1,3},{2,0},{3,1},{4,6},{5,7},{6,4},{7,5},{8,10},{9,11},{10,... | collective-permute-start | bytes 786440 | tf_op jit(solution)/shard_map/ppermute | solution.py:14
  10.4 7.6 %collective-permute-start.4 = (bf16[256,512]{1,0:T(8,128)(2,1)S(1)}, bf16[256,512]{1,0:T(8,128)(2,1)S(1)}, u32[]{:S(2)}, u32[]{:S(2)}) collective-permute-start(bf16[256,512]{1,0:T(8,128)(2,1)S(1)} %broadcast_multiply_fusion.1.refs_0_.refs_4_), channel_id=1, source_target_pairs={{0,4},{4,0},{8,12},{12,8},{16,20},{20,16},{24,28},{28,24},{1,5},{5... | collective-permute-start | bytes 786440 | tf_op jit(solution)/shard_map/ppermute | solution.py:14
  18.1 3.8 %collective-permute-start.6 = (bf16[256,512]{1,0:T(8,128)(2,1)S(1)}, bf16[256,512]{1,0:T(8,128)(2,1)S(1)}, u32[]{:S(2)}, u32[]{:S(2)}) collective-permute-start(bf16[256,512]{1,0:T(8,128)(2,1)S(1)} %broadcast_multiply_fusion.1.refs_0_.refs_4_), channel_id=1, source_target_pairs={{8,16},{12,20},{16,8},{20,12},{9,17},{13,21},{17,9},{21,13},{10,18... | collective-permute-start | bytes 786440 | tf_op jit(solution)/shard_map/ppermute | solution.py:18
  18.7 9.6 %collective-permute-start.10 = (bf16[256,512]{1,0:T(8,128)(2,1)S(1)}, bf16[256,512]{1,0:T(8,128)(2,1)S(1)}, u32[]{:S(2)}, u32[]{:S(2)}) collective-permute-start(bf16[256,512]{1,0:T(8,128)(2,1)S(1)} %collective-permute-done.refs_6_), channel_id=1, source_target_pairs={{8,0},{12,4},{16,24},{20,28},{9,1},{13,5},{17,25},{21,29},{10,2},{... | collective-permute-start | bytes 786440 | tf_op jit(solution)/shard_map/ppermute | solution.py:18
  20.0 8.4 %collective-permute-start.8 = (bf16[256,512]{1,0:T(8,128)(2,1)S(1)}, bf16[256,512]{1,0:T(8,128)(2,1)S(1)}, u32[]{:S(2)}, u32[]{:S(2)}) collective-permute-start(bf16[256,512]{1,0:T(8,128)(2,1)S(1)} %collective-permute-done.refs_6_), channel_id=1, source_target_pairs={{0,4},{4,0},{8,12},{12,8},{16,20},{20,16},{24,28},{28,24},{1,5},{5... | collective-permute-start | bytes 786440 | tf_op jit(solution)/shard_map/ppermute | solution.py:14
  20.1 8.7 %collective-permute-start.5 = (bf16[256,512]{1,0:T(8,128)(2,1)S(1)}, bf16[256,512]{1,0:T(8,128)(2,1)S(1)}, u32[]{:S(2)}, u32[]{:S(2)}) collective-permute-start(bf16[256,512]{1,0:T(8,128)(2,1)S(1)} %collective-permute-done.3.refs_2_), channel_id=1, source_target_pairs={{0,1},{1,0},{2,3},{3,2},{4,5},{5,4},{6,7},{7,6},{8,9},{9,8},{10,11... | collective-permute-start | bytes 786440 | tf_op jit(solution)/shard_map/ppermute | solution.py:14
  21.7 7.1 %collective-permute-start.7 = (bf16[256,512]{1,0:T(8,128)(2,1)S(1)}, bf16[256,512]{1,0:T(8,128)(2,1)S(1)}, u32[]{:S(2)}, u32[]{:S(2)}) collective-permute-start(bf16[256,512]{1,0:T(8,128)(2,1)S(1)} %collective-permute-done.1.refs_5_), channel_id=1, source_target_pairs={{0,4},{4,0},{8,12},{12,8},{16,20},{20,16},{24,28},{28,24},{1,5},{5... | collective-permute-start | bytes 786440 | tf_op jit(solution)/shard_map/ppermute | solution.py:14
  21.9 7.0 %collective-permute-start.9 = (bf16[256,512]{1,0:T(8,128)(2,1)S(1)}, bf16[256,512]{1,0:T(8,128)(2,1)S(1)}, u32[]{:S(2)}, u32[]{:S(2)}) collective-permute-start(bf16[256,512]{1,0:T(8,128)(2,1)S(1)} %collective-permute-done.6.refs_7_), channel_id=1, source_target_pairs={{0,4},{4,0},{8,12},{12,8},{16,20},{20,16},{24,28},{28,24},{1,5},{5... | collective-permute-start | bytes 786440 | tf_op jit(solution)/shard_map/ppermute | solution.py:14
  28.4 1.8 %collective-permute-start.11 = (bf16[256,512]{1,0:T(8,128)(2,1)S(1)}, bf16[256,512]{1,0:T(8,128)(2,1)S(1)}, u32[]{:S(2)}, u32[]{:S(2)}) collective-permute-start(bf16[256,512]{1,0:T(8,128)(2,1)S(1)} %collective-permute-done.10.own), channel_id=1, source_target_pairs={{0,4},{4,0},{8,12},{12,8},{16,20},{20,16},{24,28},{28,24},{1,5},{5... | collective-permute-start | bytes 786440 | tf_op jit(solution)/shard_map/ppermute | solution.py:14
  30.2 0.7 %copy-start = (s32[1,2]{1,0:T(1,128)S(1)}, s32[1,2]{1,0:T(1,128)}, u32[]{:S(2)}) copy-start(s32[1,2]{1,0:T(1,128)} %keep.1) | copy-start | bytes 28
  31.7 1.2 %collective-permute-start.12 = (f32[1,512]{1,0:T(1,128)S(1)}, f32[1,512]{1,0:T(1,128)S(1)}, u32[]{:S(2)}, u32[]{:S(2)}) collective-permute-start(f32[1,512]{1,0:T(1,128)S(1)} %get-tuple-element.24), channel_id=1, source_target_pairs={{0,4},{4,0},{8,12},{12,8},{16,20},{20,16},{24,28},{28,24},{1,5},{5... | collective-permute-start | bytes 6152 | tf_op jit(solution)/shard_map/ppermute | solution.py:14
  32.9 4.8 %collective-permute-start.13 = (f32[1,512]{1,0:T(1,128)S(1)}, f32[1,512]{1,0:T(1,128)S(1)}, u32[]{:S(2)}, u32[]{:S(2)}) collective-permute-start(f32[1,512]{1,0:T(1,128)S(1)} %add.15), channel_id=1, source_target_pairs={{0,8},{4,12},{8,0},{12,4},{16,24},{20,28},{24,16},{28,20},{1,9},{5... | collective-permute-start | bytes 6152 | tf_op jit(solution)/shard_map/ppermute | solution.py:14
  37.7 4.8 %collective-permute-start.14 = (f32[1,512]{1,0:T(1,128)S(1)}, f32[1,512]{1,0:T(1,128)S(1)}, u32[]{:S(2)}, u32[]{:S(2)}) collective-permute-start(f32[1,512]{1,0:T(1,128)S(1)} %add.16), channel_id=1, source_target_pairs={{0,16},{4,20},{8,24},{12,28},{16,0},{20,4},{24,8},{28,12},{1,17},{... | collective-permute-start | bytes 6152 | tf_op jit(solution)/shard_map/ppermute | solution.py:14

commit v3 on v2

v3 whole, which is shorter than its diff:
```python
import functools

import jax
import jax.numpy as jnp
from jax import lax
from jax.experimental import pallas as pl
from jax.experimental.pallas import tpu as pltpu
from jax.sharding import PartitionSpec as P

BS = 256
HALF = BS // 2
SMEM = pl.BlockSpec(memory_space=pltpu.SMEM)
VMEM = pl.BlockSpec(memory_space=pltpu.VMEM)


def swap(value, axis, size, mask):
    return lax.ppermute(value, axis, [(i, i ^ mask) for i in range(size)])


def along_z(value, pairs):
    return lax.ppermute(value, "row", [(2 * s + k, 2 * t + k) for s, t in pairs for k in (0, 1)])


def after(value, *others):
    return lax.optimization_barrier((value, *others))[0]


def resident(value):
    return pltpu.with_memory_space_constraint(value, pltpu.VMEM)


def mask_kernel(live_hbm, keep_hbm, similarity_hbm, *rest):
    *blocks, keep, live, similarity, sems = rest
    copies = [
        pltpu.make_async_copy(similarity_hbm, similarity, sems.at[0]),
        pltpu.make_async_copy(live_hbm, live, sems.at[1]),
        pltpu.make_async_copy(keep_hbm, keep, sems.at[2]),
    ]
    for copy in copies:
        copy.start()
    for copy in copies[::-1]:
        copy.wait()
    for b in range(similarity.shape[1] // BS):
        cols = slice(b * BS, (b + 1) * BS)
        kept = similarity[:, cols]
        kept = jnp.where(live[0, b] != 0, kept, jnp.zeros_like(kept))
        for (first, count), block in zip(split(len(blocks)), blocks):
            block[:, cols] = kept[first : first + count]


def split(blocks):
    return [(0, BS), (0, HALF), (HALF, HALF)][:blocks]


def masked(similarity, in_mask, out_mask, halves):
    cols = similarity.shape[1]
    shapes = [pltpu.VMEM((n, cols), jnp.bfloat16) for _, n in split(3 if halves else 1)]
    hbm = pl.BlockSpec(memory_space=pltpu.HBM)
    operands = [in_mask, out_mask, similarity]
    return pl.pallas_call(
        mask_kernel,
        out_shape=shapes + [pltpu.SMEM(out_mask.shape, jnp.int32)],
        in_specs=[hbm] * 3,
        out_specs=[VMEM] * len(shapes) + [SMEM],
        scratch_shapes=[
            pltpu.SMEM(in_mask.shape, jnp.int32),
            pltpu.VMEM(similarity.shape, jnp.bfloat16),
            pltpu.SemaphoreType.DMA((3,)),
        ],
        compiler_params=pltpu.CompilerParams(vmem_limit_bytes=16 * BS * cols),
    )(*[pltpu.with_memory_space_constraint(value, pltpu.HBM) for value in operands])


def term(panel, core, first, own, other):
    rows = own.shape[0]
    here = pl.ds(pl.multiple_of(core * BS + first, HALF), rows)
    there = pl.ds(pl.multiple_of((1 - core) * BS + first, HALF), rows)
    return jnp.dot(
        panel[:, here], own[...], preferred_element_type=jnp.float32
    ) + jnp.dot(panel[:, there], other[...], preferred_element_type=jnp.float32)


def early_kernel(n_col, pieces, last, *refs):
    panels = refs[:n_col]
    mine = refs[n_col : n_col + len(pieces)]
    theirs = refs[n_col + len(pieces) : n_col + 2 * len(pieces)]
    acc_ref, late_ref, slots = refs[n_col + 2 * len(pieces) :]
    row, col = lax.axis_index("row"), lax.axis_index("col")
    z, core = row // 2, row % 2
    for j in range(n_col):
        slots[col ^ j] = panels[j][...]
    acc = None
    for (m, first), own, other in zip(pieces, mine, theirs):
        part = term(slots.at[z ^ m], core, first, own, other)
        acc = part if acc is None else acc + part
    acc_ref[...] = acc
    late_ref[...] = slots[z ^ last]


def late_kernel(first, keep, acc_ref, panel, own, other, out_ref, sums_ref):
    core = lax.axis_index("row") % 2
    product = acc_ref[...] + term(panel, core, first, own, other)
    for b in range(product.shape[1] // BS):
        cols = slice(b * BS, (b + 1) * BS)
        kept = jnp.where(keep[0, b] != 0, product[:, cols], 0.0)
        inflated = kept * kept
        out_ref[:, cols] = inflated
        sums_ref[:, cols] = jnp.sum(inflated, axis=0, keepdims=True)


def gather_line(sparse, halves, n_row, n_col):
    two = [(i, i ^ 2) for i in range(4)]
    out = [(1, 0), (2, 3)]

    def share(value, *others):
        return swap(after(value, *others) if others else value, "row", n_row, 1)

    top = along_z(halves[0], two)
    own = share(sparse, top)
    x = swap(sparse, "col", n_col, 1)
    y = swap(sparse, "col", n_col, 2)
    one = along_z(sparse, [(i, i ^ 1) for i in range(4)])
    bottom = along_z(halves[1], two)
    far_top = along_z(after(top, x), out)
    middle = along_z(after(sparse, top, x, y), [(1, 2), (2, 1)])
    xy = swap(after(y, top), "col", n_col, 1)
    ones = share(one)
    far_bottom = along_z(bottom, out)
    tops = share(top, bottom, far_top)
    bottoms = share(bottom, far_top, xy)
    middles = share(middle)
    far_tops = share(far_top)
    far_bottoms = share(far_bottom, y)
    return [sparse, x, y, xy], [
        (2, 0, top, tops),
        (3, 0, middle, middles),
        (1, 0, one, ones),
        (3, 0, far_top, far_tops),
        (0, 0, sparse, own),
        (2, HALF, bottom, bottoms),
        (3, HALF, far_bottom, far_bottoms),
    ]


def gather(sparse, n_row, n_col):
    panels = [sparse]
    while len(panels) < n_col:
        panels += [swap(panel, "col", n_col, len(panels)) for panel in panels]
    blocks = [sparse] + [swap(sparse, "row", n_row, 2 * m) for m in range(1, n_row // 2)]
    return panels, [(m, 0, own, swap(own, "row", n_row, 1)) for m, own in enumerate(blocks)]


def on_device(n_row, n_col, similarity, in_mask, out_mask):
    rows_loc, cols_loc = similarity.shape
    line = (n_row, n_col) == (8, 4)
    sparse, *halves, keep = masked(similarity, in_mask, out_mask, line)
    if line:
        panels, pieces = gather_line(sparse, halves, n_row, n_col)
    else:
        panels, pieces = gather(sparse, n_row, n_col)
    where = [(m, first) for m, first, _, _ in pieces]
    mine = [own for _, _, own, _ in pieces]
    theirs = [other for _, _, _, other in pieces]

    size = 2 * rows_loc * cols_loc
    operands = panels + mine[:-1] + theirs[:-1]
    acc, late_panel = pl.pallas_call(
        functools.partial(early_kernel, n_col, where[:-1], where[-1][0]),
        out_shape=(
            pltpu.VMEM((rows_loc, cols_loc), jnp.float32),
            pltpu.VMEM((rows_loc, cols_loc), jnp.bfloat16),
        ),
        in_specs=[VMEM] * len(operands),
        out_specs=(VMEM, VMEM),
        scratch_shapes=[pltpu.VMEM((n_col, rows_loc, cols_loc), jnp.bfloat16)],
        compiler_params=pltpu.CompilerParams(vmem_limit_bytes=(n_col + 8) * size),
    )(*map(resident, operands))
    inflated, sums = pl.pallas_call(
        functools.partial(late_kernel, where[-1][1]),
        out_shape=(
            pltpu.VMEM((rows_loc, cols_loc), jnp.float32),
            pltpu.VMEM((1, cols_loc), jnp.float32),
        ),
        in_specs=[SMEM] + [VMEM] * 4,
        out_specs=(VMEM, VMEM),
        compiler_params=pltpu.CompilerParams(vmem_limit_bytes=8 * size),
    )(keep, acc, late_panel, resident(mine[-1]), resident(theirs[-1]))

    step = 1
    while step < n_row:
        sums = sums + swap(sums, "row", n_row, step)
        step *= 2
    total = jnp.float32(rows_loc * n_row)
    return inflated * (total / sums)


def solution(mesh):
    in_specs = (P("row", "col"), P("row", "col"), P("row", "col"))
    out_specs = P("row", "col")
    body = functools.partial(on_device, mesh.shape["row"], mesh.shape["col"])
    return jax.shard_map(
        body, mesh=mesh, in_specs=in_specs, out_specs=out_specs, check_vma=False
    )
```

time: 43.6 us -> 39.7 us (0.911)
  starting transfers between devices: 19.5 us -> 17.6 us
  other arithmetic: 2.58 us -> 0.87 us
  local copies, waits for them, and re-layouts: 0.73 us -> 0 us
    ppermute x11 -> x13, waiting for transfers between devices: 4.54 us -> 6.83 us  [swap(): return lax.ppermute(value, axis, [(i, i ^ mask) for i in range(size)])]
    ppermute x11 -> x13, starting transfers between devices: 11.9 us -> 9.85 us  [swap(): return lax.ppermute(value, axis, [(i, i ^ mask) for i in range(size)])]
    ppermute x4 -> x6, waiting for transfers between devices: 13.8 us -> 11.9 us  [along_z(): lax.ppermute(value, 'row', [(2 * s + k, 2 * t + k) for s, t in pairs for...]
    mul x2 -> x0, other arithmetic: 1.63 us -> none  [on_device(): similarity.reshape(rblocks, BS, cblocks, BS) * live]
    unnamed x4 -> x0, local copies, waits for them, and re-layouts: 0.73 us -> none
    pallas_call x2 -> x3, Pallas kernels: 2.15 us -> 2.32 us  [the longest x1 1.02 us: on_device(): pl.pallas_call(functools.partial(early_kernel, n_col, where[:-1], where[-...]
    ppermute x4 -> x6, starting transfers between devices: 7.65 us -> 7.73 us  [along_z(): lax.ppermute(value, 'row', [(2 * s + k, 2 * t + k) for s, t in pairs for...]
  transfers between devices with their start and end apart: 15 -> 19, of which waited for: 7 -> 11; matrix products, arithmetic and copies ran while one was open for 0% -> 0% of each run, Pallas kernels for 3% -> 3%
where the time goes in v3:
time: 39.7 us; the launch traced here: 39.6 us
  waiting for transfers between devices  18.7 us (47%)
  starting transfers between devices  17.6 us (44%)
  Pallas kernels  2.32 us (6%)
  other arithmetic  0.87 us (2%)
    ppermute x6, waiting for transfers between devices, along_z(): lax.ppermute(value, 'row', [(2 * s + k, 2 * t + k) for s, t in pairs for...  11.9 us
    ppermute x13, starting transfers between devices, swap(): return lax.ppermute(value, axis, [(i, i ^ mask) for i in range(size)])  9.85 us
    ppermute x6, starting transfers between devices, along_z(): lax.ppermute(value, 'row', [(2 * s + k, 2 * t + k) for s, t in pairs for...  7.73 us
    ppermute x13, waiting for transfers between devices, swap(): return lax.ppermute(value, axis, [(i, i ^ mask) for i in range(size)])  6.83 us
    pallas_call x1, Pallas kernels, on_device(): pl.pallas_call(functools.partial(early_kernel, n_col, where[:-1], where[-...  1.02 us
    pallas_call x1, Pallas kernels, masked(): pl.pallas_call(mask_kernel, out_shape=shapes + [pltpu.SMEM(out_mask.shape...  1.01 us
    mul x1, other arithmetic, on_device(): return inflated * (total / sums)  0.86 us
  transfers between devices with their start and end apart: 19, of which 11 were waited for; matrix products, arithmetic and copies ran while one was open for 0% of the time, Pallas kernels for 3%

profile of v3, /device:TPU:0, one launch (start us, length us, event | category | flops | bytes accessed | tf_op | source)
XLA Modules:
  0.0 39.6 jit_solution(16732064484009859245)
XLA Ops:
  0.0 1.0 %shard_map.37 = (bf16[256,512]{1,0:T(8,128)(2,1)S(1)}, bf16[128,512]{1,0:T(8,128)(2,1)S(1)}, bf16[128,512]{1,0:T(8,128)(2,1)S(1)}, s32[1,2]{1,0:T(1,128)S(4)}) custom-call(s32[1,2]{1,0:T(1,128)} %live_hbm.1, s32[1,2]{1,0:T(1,128)} %keep_hbm.1, bf16[256,512]{1,0:T(8,128)(2,1)} %similarity_hbm.1), custom_call_target="tpu_custom_call" | custom-call | tf_op jit(solution)/shard_map/pallas_call | solution.py:60
  1.0 3.0 %collective-permute-start = (bf16[256,512]{1,0:T(8,128)(2,1)S(1)}, bf16[256,512]{1,0:T(8,128)(2,1)S(1)}, u32[]{:S(2)}, u32[]{:S(2)}) collective-permute-start(bf16[256,512]{1,0:T(8,128)(2,1)S(1)} %get-tuple-element.28.refs_0_.refs_8_), channel_id=1, source_target_pairs={{0,1},{1,0},{2,3},{3,2},{4,5},{5,4},{6,7},{7,6},{8,9},{9,8},{10,11... | collective-permute-start | bytes 786440 | tf_op jit(solution)/shard_map/ppermute | solution.py:17
  4.0 1.5 %collective-permute-start.1 = (bf16[256,512]{1,0:T(8,128)(2,1)S(1)}, bf16[256,512]{1,0:T(8,128)(2,1)S(1)}, u32[]{:S(2)}, u32[]{:S(2)}) collective-permute-start(bf16[256,512]{1,0:T(8,128)(2,1)S(1)} %get-tuple-element.28.refs_0_.refs_8_), channel_id=1, source_target_pairs={{0,2},{1,3},{2,0},{3,1},{4,6},{5,7},{6,4},{7,5},{8,10},{9,11},{10,... | collective-permute-start | bytes 786440 | tf_op jit(solution)/shard_map/ppermute | solution.py:17
  5.5 2.6 %collective-permute-start.2 = (bf16[128,512]{1,0:T(8,128)(2,1)S(1)}, bf16[128,512]{1,0:T(8,128)(2,1)S(1)}, u32[]{:S(2)}, u32[]{:S(2)}) collective-permute-start(bf16[128,512]{1,0:T(8,128)(2,1)S(1)} %get-tuple-element.22), channel_id=1, source_target_pairs={{0,16},{4,20},{8,24},{12,28},{16,0},{20,4},{24,8},{28,12},{1,17},{... | collective-permute-start | bytes 393224 | tf_op jit(solution)/shard_map/ppermute | solution.py:21
  8.1 1.6 %collective-permute-start.5 = (bf16[256,512]{1,0:T(8,128)(2,1)S(1)}, bf16[256,512]{1,0:T(8,128)(2,1)S(1)}, u32[]{:S(2)}, u32[]{:S(2)}) collective-permute-start(bf16[256,512]{1,0:T(8,128)(2,1)S(1)} %get-tuple-element.28.refs_0_.refs_8_), channel_id=1, source_target_pairs={{0,8},{4,12},{8,0},{12,4},{16,24},{20,28},{24,16},{28,20},{1,9},{5... | collective-permute-start | bytes 786440 | tf_op jit(solution)/shard_map/ppermute | solution.py:21
  9.7 0.3 collective-permute-start.7
  10.0 4.9 %collective-permute-done.2.refs_4_ = bf16[128,512]{1,0:T(8,128)(2,1)S(1)} collective-permute-done((bf16[128,512]{1,0:T(8,128)(2,1)S(1)}, bf16[128,512]{1,0:T(8,128)(2,1)S(1)}, u32[]{:S(2)}, u32[]{:S(2)}) %collective-permute-start.2) | collective-permute-done | bytes 131104 | tf_op jit(solution)/shard_map/ppermute | solution.py:21
  14.9 0.0 collective-permute-done.refs_1_
  14.9 0.0 collective-permute-done.1.refs_2_
  14.9 0.7 %collective-permute-start.4 = (bf16[256,512]{1,0:T(8,128)(2,1)S(1)}, bf16[256,512]{1,0:T(8,128)(2,1)S(1)}, u32[]{:S(2)}, u32[]{:S(2)}) collective-permute-start(bf16[256,512]{1,0:T(8,128)(2,1)S(1)} %get-tuple-element.28.refs_0_.refs_8_), channel_id=1, source_target_pairs={{8,16},{12,20},{16,8},{20,12},{9,17},{13,21},{17,9},{21,13},{10,18... | collective-permute-start | bytes 786440 | tf_op jit(solution)/shard_map/ppermute | solution.py:21
  15.6 0.6 %collective-permute-start.3 = (bf16[256,512]{1,0:T(8,128)(2,1)S(1)}, bf16[256,512]{1,0:T(8,128)(2,1)S(1)}, u32[]{:S(2)}, u32[]{:S(2)}) collective-permute-start(bf16[256,512]{1,0:T(8,128)(2,1)S(1)} %collective-permute-done.1.refs_2_), channel_id=1, source_target_pairs={{0,1},{1,0},{2,3},{3,2},{4,5},{5,4},{6,7},{7,6},{8,9},{9,8},{10,11... | collective-permute-start | bytes 786440 | tf_op jit(solution)/shard_map/ppermute | solution.py:17
  16.2 1.3 %collective-permute-start.6 = (bf16[128,512]{1,0:T(8,128)(2,1)S(1)}, bf16[128,512]{1,0:T(8,128)(2,1)S(1)}, u32[]{:S(2)}, u32[]{:S(2)}) collective-permute-start(bf16[128,512]{1,0:T(8,128)(2,1)S(1)} %collective-permute-done.2.refs_4_), channel_id=1, source_target_pairs={{8,0},{12,4},{16,24},{20,28},{9,1},{13,5},{17,25},{21,29},{10,2},{... | collective-permute-start | bytes 393224 | tf_op jit(solution)/shard_map/ppermute | solution.py:21
  17.5 1.3 %collective-permute-done.7.refs_9_ = bf16[128,512]{1,0:T(8,128)(2,1)S(1)} collective-permute-done((bf16[128,512]{1,0:T(8,128)(2,1)S(1)}, bf16[128,512]{1,0:T(8,128)(2,1)S(1)}, u32[]{:S(2)}, u32[]{:S(2)}) %collective-permute-start.7) | collective-permute-done | bytes 131104 | tf_op jit(solution)/shard_map/ppermute | solution.py:21
  18.8 1.3 %collective-permute-start.14 = (bf16[128,512]{1,0:T(8,128)(2,1)S(1)}, bf16[128,512]{1,0:T(8,128)(2,1)S(1)}, u32[]{:S(2)}, u32[]{:S(2)}) collective-permute-start(bf16[128,512]{1,0:T(8,128)(2,1)S(1)} %collective-permute-done.7.refs_9_), channel_id=1, source_target_pairs={{8,0},{12,4},{16,24},{20,28},{9,1},{13,5},{17,25},{21,29},{10,2},{... | collective-permute-start | bytes 393224 | tf_op jit(solution)/shard_map/ppermute | solution.py:21
  20.1 1.0 %collective-permute-done.5.refs_6_ = bf16[256,512]{1,0:T(8,128)(2,1)S(1)} collective-permute-done((bf16[256,512]{1,0:T(8,128)(2,1)S(1)}, bf16[256,512]{1,0:T(8,128)(2,1)S(1)}, u32[]{:S(2)}, u32[]{:S(2)}) %collective-permute-start.5) | collective-permute-done | bytes 262176 | tf_op jit(solution)/shard_map/ppermute | solution.py:21
  21.1 0.0 collective-permute-start.12
  21.1 3.3 %collective-permute-done.6.refs_7_ = bf16[128,512]{1,0:T(8,128)(2,1)S(1)} collective-permute-done((bf16[128,512]{1,0:T(8,128)(2,1)S(1)}, bf16[128,512]{1,0:T(8,128)(2,1)S(1)}, u32[]{:S(2)}, u32[]{:S(2)}) %collective-permute-start.6) | collective-permute-done | bytes 131104 | tf_op jit(solution)/shard_map/ppermute | solution.py:21
  24.4 0.0 collective-permute-start.10
  24.4 1.4 %collective-permute-done.14.own = bf16[128,512]{1,0:T(8,128)(2,1)S(1)} collective-permute-done((bf16[128,512]{1,0:T(8,128)(2,1)S(1)}, bf16[128,512]{1,0:T(8,128)(2,1)S(1)}, u32[]{:S(2)}, u32[]{:S(2)}) %collective-permute-start.14) | collective-permute-done | bytes 131104 | tf_op jit(solution)/shard_map/ppermute | solution.py:21
  25.8 0.0 collective-permute-start.8
  25.8 0.0 collective-permute-done.4.refs_5_
  25.8 0.5 %collective-permute-start.9 = (bf16[256,512]{1,0:T(8,128)(2,1)S(1)}, bf16[256,512]{1,0:T(8,128)(2,1)S(1)}, u32[]{:S(2)}, u32[]{:S(2)}) collective-permute-start(bf16[256,512]{1,0:T(8,128)(2,1)S(1)} %collective-permute-done.4.refs_5_), channel_id=1, source_target_pairs={{0,4},{4,0},{8,12},{12,8},{16,20},{20,16},{24,28},{28,24},{1,5},{5... | collective-permute-start | bytes 786440 | tf_op jit(solution)/shard_map/ppermute | solution.py:17
  26.3 0.0 collective-permute-done.3.refs_3_
  26.3 0.1 collective-permute-start.11
  26.4 0.0 collective-permute-done.12.refs_14_
  26.4 0.4 %collective-permute-start.13 = (bf16[128,512]{1,0:T(8,128)(2,1)S(1)}, bf16[128,512]{1,0:T(8,128)(2,1)S(1)}, u32[]{:S(2)}, u32[]{:S(2)}) collective-permute-start(bf16[128,512]{1,0:T(8,128)(2,1)S(1)} %collective-permute-done.7.refs_9_), channel_id=1, source_target_pairs={{0,4},{4,0},{8,12},{12,8},{16,20},{20,16},{24,28},{28,24},{1,5},{5... | collective-permute-start | bytes 393224 | tf_op jit(solution)/shard_map/ppermute | solution.py:17
  26.8 0.3 collective-permute-done.8.refs_10_
  27.1 0.1 collective-permute-start.15
  27.3 0.0 collective-permute-done.10.refs_12_
  27.3 0.4 %collective-permute-done.11.refs_13_ = bf16[128,512]{1,0:T(8,128)(2,1)S(1)} collective-permute-done((bf16[128,512]{1,0:T(8,128)(2,1)S(1)}, bf16[128,512]{1,0:T(8,128)(2,1)S(1)}, u32[]{:S(2)}, u32[]{:S(2)}) %collective-permute-start.11) | collective-permute-done | bytes 131104 | tf_op jit(solution)/shard_map/ppermute | solution.py:17
  27.7 0.2 collective-permute-done.13.refs_15_
  27.9 0.0 collective-permute-done.9.refs_11_
  27.9 1.0 %shard_map.38 = (f32[256,512]{1,0:T(8,128)S(1)}, bf16[256,512]{1,0:T(8,128)(2,1)S(1)}) custom-call(bf16[256,512]{1,0:T(8,128)(2,1)S(1)} %get-tuple-element.28.refs_0_.refs_8_, bf16[256,512]{1,0:T(8,128)(2,1)S(1)} %collective-permute-done.refs_1_, bf16[256,512]{1,0:T(8,128)(2,1)S(1)} %collective-permute-done.1.refs_2_, ...), custom_call_target="tpu_custom_call" | custom-call | tf_op jit(solution)/shard_map/pallas_call | solution.py:167
  28.9 0.0 collective-permute-done.15.other
  28.9 0.3 shard_map.39
  29.2 0.4 collective-permute-start.16
  29.6 0.8 %collective-permute-done.16 = f32[1,512]{1,0:T(1,128)S(1)} collective-permute-done((f32[1,512]{1,0:T(1,128)S(1)}, f32[1,512]{1,0:T(1,128)S(1)}, u32[]{:S(2)}, u32[]{:S(2)}) %collective-permute-start.16) | collective-permute-done | bytes 2080 | tf_op jit(solution)/shard_map/ppermute | solution.py:17
  30.5 0.1 collective-permute-start.17
  30.5 3.5 %collective-permute-done.17 = f32[1,512]{1,0:T(1,128)S(1)} collective-permute-done((f32[1,512]{1,0:T(1,128)S(1)}, f32[1,512]{1,0:T(1,128)S(1)}, u32[]{:S(2)}, u32[]{:S(2)}) %collective-permute-start.17) | collective-permute-done | bytes 2080 | tf_op jit(solution)/shard_map/ppermute | solution.py:17
  34.1 3.1 %collective-permute-start.18 = (f32[1,512]{1,0:T(1,128)S(1)}, f32[1,512]{1,0:T(1,128)S(1)}, u32[]{:S(2)}, u32[]{:S(2)}) collective-permute-start(f32[1,512]{1,0:T(1,128)S(1)} %add.10), channel_id=1, source_target_pairs={{0,16},{4,20},{8,24},{12,28},{16,0},{20,4},{24,8},{28,12},{1,17},{... | collective-permute-start | bytes 6152 | tf_op jit(solution)/shard_map/ppermute | solution.py:17
  37.1 1.6 %collective-permute-done.18 = f32[1,512]{1,0:T(1,128)S(1)} collective-permute-done((f32[1,512]{1,0:T(1,128)S(1)}, f32[1,512]{1,0:T(1,128)S(1)}, u32[]{:S(2)}, u32[]{:S(2)}) %collective-permute-start.18) | collective-permute-done | bytes 2080 | tf_op jit(solution)/shard_map/ppermute | solution.py:17
  38.7 0.9 %broadcast_multiply_fusion = f32[256,512]{1,0:T(8,128)} fusion(f32[256,512]{1,0:T(8,128)S(1)} %get-tuple-element.33, f32[512]{0:T(512)S(1)} %bitcast.1), kind=kLoop, calls=%fused_computation | loop fusion | flops 131072 | bytes 1050624 | tf_op jit(solution)/shard_map/mul | solution.py:194
  (3 shorter events, 0.0 us)
Async XLA Ops:
  1.0 13.9 %collective-permute-start = (bf16[256,512]{1,0:T(8,128)(2,1)S(1)}, bf16[256,512]{1,0:T(8,128)(2,1)S(1)}, u32[]{:S(2)}, u32[]{:S(2)}) collective-permute-start(bf16[256,512]{1,0:T(8,128)(2,1)S(1)} %get-tuple-element.28.refs_0_.refs_8_), channel_id=1, source_target_pairs={{0,1},{1,0},{2,3},{3,2},{4,5},{5,4},{6,7},{7,6},{8,9},{9,8},{10,11... | collective-permute-start | bytes 786440 | tf_op jit(solution)/shard_map/ppermute | solution.py:17
  4.0 10.9 %collective-permute-start.1 = (bf16[256,512]{1,0:T(8,128)(2,1)S(1)}, bf16[256,512]{1,0:T(8,128)(2,1)S(1)}, u32[]{:S(2)}, u32[]{:S(2)}) collective-permute-start(bf16[256,512]{1,0:T(8,128)(2,1)S(1)} %get-tuple-element.28.refs_0_.refs_8_), channel_id=1, source_target_pairs={{0,2},{1,3},{2,0},{3,1},{4,6},{5,7},{6,4},{7,5},{8,10},{9,11},{10,... | collective-permute-start | bytes 786440 | tf_op jit(solution)/shard_map/ppermute | solution.py:17
  5.5 9.4 %collective-permute-start.2 = (bf16[128,512]{1,0:T(8,128)(2,1)S(1)}, bf16[128,512]{1,0:T(8,128)(2,1)S(1)}, u32[]{:S(2)}, u32[]{:S(2)}) collective-permute-start(bf16[128,512]{1,0:T(8,128)(2,1)S(1)} %get-tuple-element.22), channel_id=1, source_target_pairs={{0,16},{4,20},{8,24},{12,28},{16,0},{20,4},{24,8},{28,12},{1,17},{... | collective-permute-start | bytes 393224 | tf_op jit(solution)/shard_map/ppermute | solution.py:21
  8.1 13.0 %collective-permute-start.5 = (bf16[256,512]{1,0:T(8,128)(2,1)S(1)}, bf16[256,512]{1,0:T(8,128)(2,1)S(1)}, u32[]{:S(2)}, u32[]{:S(2)}) collective-permute-start(bf16[256,512]{1,0:T(8,128)(2,1)S(1)} %get-tuple-element.28.refs_0_.refs_8_), channel_id=1, source_target_pairs={{0,8},{4,12},{8,0},{12,4},{16,24},{20,28},{24,16},{28,20},{1,9},{5... | collective-permute-start | bytes 786440 | tf_op jit(solution)/shard_map/ppermute | solution.py:21
  9.7 9.1 %collective-permute-start.7 = (bf16[128,512]{1,0:T(8,128)(2,1)S(1)}, bf16[128,512]{1,0:T(8,128)(2,1)S(1)}, u32[]{:S(2)}, u32[]{:S(2)}) collective-permute-start(bf16[128,512]{1,0:T(8,128)(2,1)S(1)} %get-tuple-element.26), channel_id=1, source_target_pairs={{0,16},{4,20},{8,24},{12,28},{16,0},{20,4},{24,8},{28,12},{1,17},{... | collective-permute-start | bytes 393224 | tf_op jit(solution)/shard_map/ppermute | solution.py:21
  14.9 10.9 %collective-permute-start.4 = (bf16[256,512]{1,0:T(8,128)(2,1)S(1)}, bf16[256,512]{1,0:T(8,128)(2,1)S(1)}, u32[]{:S(2)}, u32[]{:S(2)}) collective-permute-start(bf16[256,512]{1,0:T(8,128)(2,1)S(1)} %get-tuple-element.28.refs_0_.refs_8_), channel_id=1, source_target_pairs={{8,16},{12,20},{16,8},{20,12},{9,17},{13,21},{17,9},{21,13},{10,18... | collective-permute-start | bytes 786440 | tf_op jit(solution)/shard_map/ppermute | solution.py:21
  15.6 10.7 %collective-permute-start.3 = (bf16[256,512]{1,0:T(8,128)(2,1)S(1)}, bf16[256,512]{1,0:T(8,128)(2,1)S(1)}, u32[]{:S(2)}, u32[]{:S(2)}) collective-permute-start(bf16[256,512]{1,0:T(8,128)(2,1)S(1)} %collective-permute-done.1.refs_2_), channel_id=1, source_target_pairs={{0,1},{1,0},{2,3},{3,2},{4,5},{5,4},{6,7},{7,6},{8,9},{9,8},{10,11... | collective-permute-start | bytes 786440 | tf_op jit(solution)/shard_map/ppermute | solution.py:17
  16.2 8.2 %collective-permute-start.6 = (bf16[128,512]{1,0:T(8,128)(2,1)S(1)}, bf16[128,512]{1,0:T(8,128)(2,1)S(1)}, u32[]{:S(2)}, u32[]{:S(2)}) collective-permute-start(bf16[128,512]{1,0:T(8,128)(2,1)S(1)} %collective-permute-done.2.refs_4_), channel_id=1, source_target_pairs={{8,0},{12,4},{16,24},{20,28},{9,1},{13,5},{17,25},{21,29},{10,2},{... | collective-permute-start | bytes 393224 | tf_op jit(solution)/shard_map/ppermute | solution.py:21
  18.8 7.0 %collective-permute-start.14 = (bf16[128,512]{1,0:T(8,128)(2,1)S(1)}, bf16[128,512]{1,0:T(8,128)(2,1)S(1)}, u32[]{:S(2)}, u32[]{:S(2)}) collective-permute-start(bf16[128,512]{1,0:T(8,128)(2,1)S(1)} %collective-permute-done.7.refs_9_), channel_id=1, source_target_pairs={{8,0},{12,4},{16,24},{20,28},{9,1},{13,5},{17,25},{21,29},{10,2},{... | collective-permute-start | bytes 393224 | tf_op jit(solution)/shard_map/ppermute | solution.py:21
  21.1 5.3 %collective-permute-start.12 = (bf16[256,512]{1,0:T(8,128)(2,1)S(1)}, bf16[256,512]{1,0:T(8,128)(2,1)S(1)}, u32[]{:S(2)}, u32[]{:S(2)}) collective-permute-start(bf16[256,512]{1,0:T(8,128)(2,1)S(1)} %get-tuple-element.28.refs_0_.refs_8_), channel_id=1, source_target_pairs={{0,4},{4,0},{8,12},{12,8},{16,20},{20,16},{24,28},{28,24},{1,5},{5... | collective-permute-start | bytes 786440 | tf_op jit(solution)/shard_map/ppermute | solution.py:17
  24.4 2.9 %collective-permute-start.10 = (bf16[256,512]{1,0:T(8,128)(2,1)S(1)}, bf16[256,512]{1,0:T(8,128)(2,1)S(1)}, u32[]{:S(2)}, u32[]{:S(2)}) collective-permute-start(bf16[256,512]{1,0:T(8,128)(2,1)S(1)} %collective-permute-done.5.refs_6_), channel_id=1, source_target_pairs={{0,4},{4,0},{8,12},{12,8},{16,20},{20,16},{24,28},{28,24},{1,5},{5... | collective-permute-start | bytes 786440 | tf_op jit(solution)/shard_map/ppermute | solution.py:17
  25.8 1.3 %collective-permute-start.8 = (bf16[128,512]{1,0:T(8,128)(2,1)S(1)}, bf16[128,512]{1,0:T(8,128)(2,1)S(1)}, u32[]{:S(2)}, u32[]{:S(2)}) collective-permute-start(bf16[128,512]{1,0:T(8,128)(2,1)S(1)} %collective-permute-done.2.refs_4_), channel_id=1, source_target_pairs={{0,4},{4,0},{8,12},{12,8},{16,20},{20,16},{24,28},{28,24},{1,5},{5... | collective-permute-start | bytes 393224 | tf_op jit(solution)/shard_map/ppermute | solution.py:17
  25.8 2.1 %collective-permute-start.9 = (bf16[256,512]{1,0:T(8,128)(2,1)S(1)}, bf16[256,512]{1,0:T(8,128)(2,1)S(1)}, u32[]{:S(2)}, u32[]{:S(2)}) collective-permute-start(bf16[256,512]{1,0:T(8,128)(2,1)S(1)} %collective-permute-done.4.refs_5_), channel_id=1, source_target_pairs={{0,4},{4,0},{8,12},{12,8},{16,20},{20,16},{24,28},{28,24},{1,5},{5... | collective-permute-start | bytes 786440 | tf_op jit(solution)/shard_map/ppermute | solution.py:17
  26.3 1.4 %collective-permute-start.11 = (bf16[128,512]{1,0:T(8,128)(2,1)S(1)}, bf16[128,512]{1,0:T(8,128)(2,1)S(1)}, u32[]{:S(2)}, u32[]{:S(2)}) collective-permute-start(bf16[128,512]{1,0:T(8,128)(2,1)S(1)} %collective-permute-done.6.refs_7_), channel_id=1, source_target_pairs={{0,4},{4,0},{8,12},{12,8},{16,20},{20,16},{24,28},{28,24},{1,5},{5... | collective-permute-start | bytes 393224 | tf_op jit(solution)/shard_map/ppermute | solution.py:17
  26.4 1.5 %collective-permute-start.13 = (bf16[128,512]{1,0:T(8,128)(2,1)S(1)}, bf16[128,512]{1,0:T(8,128)(2,1)S(1)}, u32[]{:S(2)}, u32[]{:S(2)}) collective-permute-start(bf16[128,512]{1,0:T(8,128)(2,1)S(1)} %collective-permute-done.7.refs_9_), channel_id=1, source_target_pairs={{0,4},{4,0},{8,12},{12,8},{16,20},{20,16},{24,28},{28,24},{1,5},{5... | collective-permute-start | bytes 393224 | tf_op jit(solution)/shard_map/ppermute | solution.py:17
  27.1 1.8 %collective-permute-start.15 = (bf16[128,512]{1,0:T(8,128)(2,1)S(1)}, bf16[128,512]{1,0:T(8,128)(2,1)S(1)}, u32[]{:S(2)}, u32[]{:S(2)}) collective-permute-start(bf16[128,512]{1,0:T(8,128)(2,1)S(1)} %collective-permute-done.14.own), channel_id=1, source_target_pairs={{0,4},{4,0},{8,12},{12,8},{16,20},{20,16},{24,28},{28,24},{1,5},{5... | collective-permute-start | bytes 393224 | tf_op jit(solution)/shard_map/ppermute | solution.py:17
  29.2 1.2 %collective-permute-start.16 = (f32[1,512]{1,0:T(1,128)S(1)}, f32[1,512]{1,0:T(1,128)S(1)}, u32[]{:S(2)}, u32[]{:S(2)}) collective-permute-start(f32[1,512]{1,0:T(1,128)S(1)} %get-tuple-element.34), channel_id=1, source_target_pairs={{0,4},{4,0},{8,12},{12,8},{16,20},{20,16},{24,28},{28,24},{1,5},{5... | collective-permute-start | bytes 6152 | tf_op jit(solution)/shard_map/ppermute | solution.py:17
  30.5 3.6 %collective-permute-start.17 = (f32[1,512]{1,0:T(1,128)S(1)}, f32[1,512]{1,0:T(1,128)S(1)}, u32[]{:S(2)}, u32[]{:S(2)}) collective-permute-start(f32[1,512]{1,0:T(1,128)S(1)} %add.9), channel_id=1, source_target_pairs={{0,8},{4,12},{8,0},{12,4},{16,24},{20,28},{24,16},{28,20},{1,9},{5... | collective-permute-start | bytes 6152 | tf_op jit(solution)/shard_map/ppermute | solution.py:17
  34.1 4.6 %collective-permute-start.18 = (f32[1,512]{1,0:T(1,128)S(1)}, f32[1,512]{1,0:T(1,128)S(1)}, u32[]{:S(2)}, u32[]{:S(2)}) collective-permute-start(f32[1,512]{1,0:T(1,128)S(1)} %add.10), channel_id=1, source_target_pairs={{0,16},{4,20},{8,24},{12,28},{16,0},{20,4},{24,8},{28,12},{1,17},{... | collective-permute-start | bytes 6152 | tf_op jit(solution)/shard_map/ppermute | solution.py:17

commit v4 on v3

--- a/solution.py
+++ b/solution.py
@@ -71,10 +71,37 @@
     )(*[pltpu.with_memory_space_constraint(value, pltpu.HBM) for value in operands])
 
 
-def term(panel, core, first, own, other):
-    rows = own.shape[0]
-    here = pl.ds(pl.multiple_of(core * BS + first, HALF), rows)
-    there = pl.ds(pl.multiple_of((1 - core) * BS + first, HALF), rows)
+def join_kernel(top, bottom, out):
+    out[:HALF] = top[...]
+    out[HALF:] = bottom[...]
+
+
+def pick_kernel(top, bottom, middle, out):
+    z = lax.axis_index("row") // 2
+    at_end = jnp.logical_or(z == 0, z == 3)
+
+    @pl.when(at_end)
+    def _():
+        join_kernel(top, bottom, out)
+
+    @pl.when(jnp.logical_not(at_end))
+    def _():
+        out[...] = middle[...]
+
+
+def joined(kernel, *blocks):
+    return pl.pallas_call(
+        kernel,
+        out_shape=pltpu.VMEM((BS, blocks[0].shape[1]), jnp.bfloat16),
+        in_specs=[VMEM] * len(blocks),
+        out_specs=VMEM,
+        compiler_params=pltpu.CompilerParams(vmem_limit_bytes=16 * BS * BS),
+    )(*map(resident, blocks))
+
+
+def term(panel, core, own, other):
+    here = pl.ds(pl.multiple_of(core * BS, BS), BS)
+    there = pl.ds(pl.multiple_of((1 - core) * BS, BS), BS)
     return jnp.dot(
         panel[:, here], own[...], preferred_element_type=jnp.float32
     ) + jnp.dot(panel[:, there], other[...], preferred_element_type=jnp.float32)
@@ -90,16 +117,16 @@
     for j in range(n_col):
         slots[col ^ j] = panels[j][...]
     acc = None
-    for (m, first), own, other in zip(pieces, mine, theirs):
-        part = term(slots.at[z ^ m], core, first, own, other)
+    for m, own, other in zip(pieces, mine, theirs):
+        part = term(slots.at[z ^ m], core, own, other)
         acc = part if acc is None else acc + part
     acc_ref[...] = acc
     late_ref[...] = slots[z ^ last]
 
 
-def late_kernel(first, keep, acc_ref, panel, own, other, out_ref, sums_ref):
+def late_kernel(keep, acc_ref, panel, own, other, out_ref, sums_ref):
     core = lax.axis_index("row") % 2
-    product = acc_ref[...] + term(panel, core, first, own, other)
+    product = acc_ref[...] + term(panel, core, own, other)
     for b in range(product.shape[1] // BS):
         cols = slice(b * BS, (b + 1) * BS)
         kept = jnp.where(keep[0, b] != 0, product[:, cols], 0.0)
@@ -116,30 +143,20 @@
         return swap(after(value, *others) if others else value, "row", n_row, 1)
 
     top = along_z(halves[0], two)
-    own = share(sparse, top)
     x = swap(sparse, "col", n_col, 1)
     y = swap(sparse, "col", n_col, 2)
     one = along_z(sparse, [(i, i ^ 1) for i in range(4)])
     bottom = along_z(halves[1], two)
-    far_top = along_z(after(top, x), out)
-    middle = along_z(after(sparse, top, x, y), [(1, 2), (2, 1)])
-    xy = swap(after(y, top), "col", n_col, 1)
-    ones = share(one)
-    far_bottom = along_z(bottom, out)
-    tops = share(top, bottom, far_top)
-    bottoms = share(bottom, far_top, xy)
-    middles = share(middle)
-    far_tops = share(far_top)
-    far_bottoms = share(far_bottom, y)
-    return [sparse, x, y, xy], [
-        (2, 0, top, tops),
-        (3, 0, middle, middles),
-        (1, 0, one, ones),
-        (3, 0, far_top, far_tops),
-        (0, 0, sparse, own),
-        (2, HALF, bottom, bottoms),
-        (3, HALF, far_bottom, far_bottoms),
-    ]
+    end_top = along_z(top, out)
+    middle = along_z(after(sparse, top, x), [(1, 2), (2, 1)])
+    xy = swap(y, "col", n_col, 1)
+    end_bottom = along_z(bottom, out)
+    own = share(sparse, xy, y)
+    ones = share(one, end_top)
+    far = joined(join_kernel, top, bottom)
+    last = joined(pick_kernel, end_top, end_bottom, middle)
+    pieces = [(2, far, share(far)), (0, sparse, own), (1, one, ones), (3, last, share(last))]
+    return [sparse, x, y, xy], pieces
 
 
 def gather(sparse, n_row, n_col):
@@ -147,7 +164,7 @@
     while len(panels) < n_col:
         panels += [swap(panel, "col", n_col, len(panels)) for panel in panels]
     blocks = [sparse] + [swap(sparse, "row", n_row, 2 * m) for m in range(1, n_row // 2)]
-    return panels, [(m, 0, own, swap(own, "row", n_row, 1)) for m, own in enumerate(blocks)]
+    return panels, [(m, own, swap(own, "row", n_row, 1)) for m, own in enumerate(blocks)]
 
 
 def on_device(n_row, n_col, similarity, in_mask, out_mask):
@@ -158,14 +175,14 @@
         panels, pieces = gather_line(sparse, halves, n_row, n_col)
     else:
         panels, pieces = gather(sparse, n_row, n_col)
-    where = [(m, first) for m, first, _, _ in pieces]
-    mine = [own for _, _, own, _ in pieces]
-    theirs = [other for _, _, _, other in pieces]
+    where = [m for m, _, _ in pieces]
+    mine = [own for _, own, _ in pieces]
+    theirs = [other for _, _, other in pieces]
 
     size = 2 * rows_loc * cols_loc
     operands = panels + mine[:-1] + theirs[:-1]
     acc, late_panel = pl.pallas_call(
-        functools.partial(early_kernel, n_col, where[:-1], where[-1][0]),
+        functools.partial(early_kernel, n_col, where[:-1], where[-1]),
         out_shape=(
             pltpu.VMEM((rows_loc, cols_loc), jnp.float32),
             pltpu.VMEM((rows_loc, cols_loc), jnp.bfloat16),
@@ -176,7 +193,7 @@
         compiler_params=pltpu.CompilerParams(vmem_limit_bytes=(n_col + 8) * size),
     )(*map(resident, operands))
     inflated, sums = pl.pallas_call(
-        functools.partial(late_kernel, where[-1][1]),
+        late_kernel,
         out_shape=(
             pltpu.VMEM((rows_loc, cols_loc), jnp.float32),
             pltpu.VMEM((1, cols_loc), jnp.float32),

time: 39.7 us -> 38.3 us (0.965)
  waiting for transfers between devices: 18.7 us -> 16.7 us
  starting transfers between devices: 17.6 us -> 18.4 us
    ppermute x6, waiting for transfers between devices: 11.9 us -> 9.7 us  [along_z(): lax.ppermute(value, 'row', [(2 * s + k, 2 * t + k) for s, t in pairs for...]
    ppermute x13 -> x10, starting transfers between devices: 9.85 us -> 10.7 us  [swap(): return lax.ppermute(value, axis, [(i, i ^ mask) for i in range(size)])]
    ppermute x13 -> x10, waiting for transfers between devices: 6.83 us -> 6.96 us  [swap(): return lax.ppermute(value, axis, [(i, i ^ mask) for i in range(size)])]
  transfers between devices with their start and end apart: 19 -> 16, of which waited for: 11 -> 10; matrix products, arithmetic and copies ran while one was open for 0% -> 0% of each run, Pallas kernels for 3% -> 2%
where the time goes in v4:
time: 38.3 us; the launch traced here: 38.1 us
  starting transfers between devices  18.4 us (48%)
  waiting for transfers between devices  16.7 us (44%)
  Pallas kernels  1.99 us (5%)
  other arithmetic  0.87 us (2%)
    ppermute x10, starting transfers between devices, swap(): return lax.ppermute(value, axis, [(i, i ^ mask) for i in range(size)])  10.7 us
    ppermute x6, waiting for transfers between devices, along_z(): lax.ppermute(value, 'row', [(2 * s + k, 2 * t + k) for s, t in pairs for...  9.7 us
    ppermute x6, starting transfers between devices, along_z(): lax.ppermute(value, 'row', [(2 * s + k, 2 * t + k) for s, t in pairs for...  7.74 us
    ppermute x10, waiting for transfers between devices, swap(): return lax.ppermute(value, axis, [(i, i ^ mask) for i in range(size)])  6.96 us
    pallas_call x1, Pallas kernels, masked(): pl.pallas_call(mask_kernel, out_shape=shapes + [pltpu.SMEM(out_mask.shape...  1.01 us
    mul x1, other arithmetic, on_device(): return inflated * (total / sums)  0.86 us
  transfers between devices with their start and end apart: 16, of which 10 were waited for; matrix products, arithmetic and copies ran while one was open for 0% of the time, Pallas kernels for 2%

profile of v4, /device:TPU:0, one launch (start us, length us, event | category | flops | bytes accessed | tf_op | source)
XLA Modules:
  0.0 38.1 jit_solution(14622372493931938768)
XLA Ops:
  0.0 1.0 %shard_map.37 = (bf16[256,512]{1,0:T(8,128)(2,1)S(1)}, bf16[128,512]{1,0:T(8,128)(2,1)S(1)}, bf16[128,512]{1,0:T(8,128)(2,1)S(1)}, s32[1,2]{1,0:T(1,128)S(4)}) custom-call(s32[1,2]{1,0:T(1,128)} %live_hbm.1, s32[1,2]{1,0:T(1,128)} %keep_hbm.1, bf16[256,512]{1,0:T(8,128)(2,1)} %similarity_hbm.1), custom_call_target="tpu_custom_call" | custom-call | tf_op jit(solution)/shard_map/pallas_call | solution.py:60
  1.0 3.0 %collective-permute-start.1 = (bf16[256,512]{1,0:T(8,128)(2,1)S(1)}, bf16[256,512]{1,0:T(8,128)(2,1)S(1)}, u32[]{:S(2)}, u32[]{:S(2)}) collective-permute-start(bf16[256,512]{1,0:T(8,128)(2,1)S(1)} %get-tuple-element.24.refs_0_.refs_5_), channel_id=1, source_target_pairs={{0,2},{1,3},{2,0},{3,1},{4,6},{5,7},{6,4},{7,5},{8,10},{9,11},{10,... | collective-permute-start | bytes 786440 | tf_op jit(solution)/shard_map/ppermute | solution.py:17
  4.1 1.5 %collective-permute-start = (bf16[256,512]{1,0:T(8,128)(2,1)S(1)}, bf16[256,512]{1,0:T(8,128)(2,1)S(1)}, u32[]{:S(2)}, u32[]{:S(2)}) collective-permute-start(bf16[256,512]{1,0:T(8,128)(2,1)S(1)} %get-tuple-element.24.refs_0_.refs_5_), channel_id=1, source_target_pairs={{0,1},{1,0},{2,3},{3,2},{4,5},{5,4},{6,7},{7,6},{8,9},{9,8},{10,11... | collective-permute-start | bytes 786440 | tf_op jit(solution)/shard_map/ppermute | solution.py:17
  5.5 2.6 %collective-permute-start.3 = (bf16[128,512]{1,0:T(8,128)(2,1)S(1)}, bf16[128,512]{1,0:T(8,128)(2,1)S(1)}, u32[]{:S(2)}, u32[]{:S(2)}) collective-permute-start(bf16[128,512]{1,0:T(8,128)(2,1)S(1)} %get-tuple-element.18), channel_id=1, source_target_pairs={{0,16},{4,20},{8,24},{12,28},{16,0},{20,4},{24,8},{28,12},{1,17},{... | collective-permute-start | bytes 393224 | tf_op jit(solution)/shard_map/ppermute | solution.py:21
  8.1 1.6 %collective-permute-start.5 = (bf16[256,512]{1,0:T(8,128)(2,1)S(1)}, bf16[256,512]{1,0:T(8,128)(2,1)S(1)}, u32[]{:S(2)}, u32[]{:S(2)}) collective-permute-start(bf16[256,512]{1,0:T(8,128)(2,1)S(1)} %get-tuple-element.24.refs_0_.refs_5_), channel_id=1, source_target_pairs={{0,8},{4,12},{8,0},{12,4},{16,24},{20,28},{24,16},{28,20},{1,9},{5... | collective-permute-start | bytes 786440 | tf_op jit(solution)/shard_map/ppermute | solution.py:21
  9.7 0.3 collective-permute-start.4
  10.0 0.3 collective-permute-done.1.refs_2_
  10.4 1.7 %collective-permute-start.2 = (bf16[256,512]{1,0:T(8,128)(2,1)S(1)}, bf16[256,512]{1,0:T(8,128)(2,1)S(1)}, u32[]{:S(2)}, u32[]{:S(2)}) collective-permute-start(bf16[256,512]{1,0:T(8,128)(2,1)S(1)} %collective-permute-done.1.refs_2_), channel_id=1, source_target_pairs={{0,1},{1,0},{2,3},{3,2},{4,5},{5,4},{6,7},{7,6},{8,9},{9,8},{10,11... | collective-permute-start | bytes 786440 | tf_op jit(solution)/shard_map/ppermute | solution.py:17
  12.1 2.9 %collective-permute-done.3.top = bf16[128,512]{1,0:T(8,128)(2,1)S(1)} collective-permute-done((bf16[128,512]{1,0:T(8,128)(2,1)S(1)}, bf16[128,512]{1,0:T(8,128)(2,1)S(1)}, u32[]{:S(2)}, u32[]{:S(2)}) %collective-permute-start.3) | collective-permute-done | bytes 131104 | tf_op jit(solution)/shard_map/ppermute | solution.py:21
  14.9 0.0 collective-permute-done.refs_1_
  14.9 0.7 %collective-permute-start.11 = (bf16[256,512]{1,0:T(8,128)(2,1)S(1)}, bf16[256,512]{1,0:T(8,128)(2,1)S(1)}, u32[]{:S(2)}, u32[]{:S(2)}) collective-permute-start(bf16[256,512]{1,0:T(8,128)(2,1)S(1)} %get-tuple-element.24.refs_0_.refs_5_), channel_id=1, source_target_pairs={{8,16},{12,20},{16,8},{20,12},{9,17},{13,21},{17,9},{21,13},{10,18... | collective-permute-start | bytes 786440 | tf_op jit(solution)/shard_map/ppermute | solution.py:21
  15.6 1.3 %collective-permute-start.8 = (bf16[128,512]{1,0:T(8,128)(2,1)S(1)}, bf16[128,512]{1,0:T(8,128)(2,1)S(1)}, u32[]{:S(2)}, u32[]{:S(2)}) collective-permute-start(bf16[128,512]{1,0:T(8,128)(2,1)S(1)} %collective-permute-done.3.top), channel_id=1, source_target_pairs={{8,0},{12,4},{16,24},{20,28},{9,1},{13,5},{17,25},{21,29},{10,2},{... | collective-permute-start | bytes 393224 | tf_op jit(solution)/shard_map/ppermute | solution.py:21
  16.9 1.9 %collective-permute-done.4.bottom = bf16[128,512]{1,0:T(8,128)(2,1)S(1)} collective-permute-done((bf16[128,512]{1,0:T(8,128)(2,1)S(1)}, bf16[128,512]{1,0:T(8,128)(2,1)S(1)}, u32[]{:S(2)}, u32[]{:S(2)}) %collective-permute-start.4) | collective-permute-done | bytes 131104 | tf_op jit(solution)/shard_map/ppermute | solution.py:21
  18.8 1.3 %collective-permute-start.10 = (bf16[128,512]{1,0:T(8,128)(2,1)S(1)}, bf16[128,512]{1,0:T(8,128)(2,1)S(1)}, u32[]{:S(2)}, u32[]{:S(2)}) collective-permute-start(bf16[128,512]{1,0:T(8,128)(2,1)S(1)} %collective-permute-done.4.bottom), channel_id=1, source_target_pairs={{8,0},{12,4},{16,24},{20,28},{9,1},{13,5},{17,25},{21,29},{10,2},{... | collective-permute-start | bytes 393224 | tf_op jit(solution)/shard_map/ppermute | solution.py:21
  20.1 3.5 %collective-permute-done.8.top = bf16[128,512]{1,0:T(8,128)(2,1)S(1)} collective-permute-done((bf16[128,512]{1,0:T(8,128)(2,1)S(1)}, bf16[128,512]{1,0:T(8,128)(2,1)S(1)}, u32[]{:S(2)}, u32[]{:S(2)}) %collective-permute-start.8) | collective-permute-done | bytes 131104 | tf_op jit(solution)/shard_map/ppermute | solution.py:21
  23.7 0.0 collective-permute-start.6
  23.7 0.0 collective-permute-done.5.refs_6_
  23.7 0.5 %collective-permute-start.9 = (bf16[256,512]{1,0:T(8,128)(2,1)S(1)}, bf16[256,512]{1,0:T(8,128)(2,1)S(1)}, u32[]{:S(2)}, u32[]{:S(2)}) collective-permute-start(bf16[256,512]{1,0:T(8,128)(2,1)S(1)} %collective-permute-done.5.refs_6_), channel_id=1, source_target_pairs={{0,4},{4,0},{8,12},{12,8},{16,20},{20,16},{24,28},{28,24},{1,5},{5... | collective-permute-start | bytes 786440 | tf_op jit(solution)/shard_map/ppermute | solution.py:17
  24.2 0.0 collective-permute-done.2.refs_3_
  24.2 0.1 collective-permute-start.7
  24.2 1.4 %collective-permute-done.10.bottom = bf16[128,512]{1,0:T(8,128)(2,1)S(1)} collective-permute-done((bf16[128,512]{1,0:T(8,128)(2,1)S(1)}, bf16[128,512]{1,0:T(8,128)(2,1)S(1)}, u32[]{:S(2)}, u32[]{:S(2)}) %collective-permute-start.10) | collective-permute-done | bytes 131104 | tf_op jit(solution)/shard_map/ppermute | solution.py:21
  25.6 0.0 collective-permute-done.11.middle
  25.7 0.1 collective-permute-start.12
  25.8 0.0 collective-permute-done.6.refs_7_
  25.8 0.0 collective-permute-done.9.refs_9_
  25.8 0.2 collective-permute-done.7.refs_8_
  25.9 0.6 %shard_map.39 = (f32[256,512]{1,0:T(8,128)S(1)}, bf16[256,512]{1,0:T(8,128)(2,1)S(1)}) custom-call(bf16[256,512]{1,0:T(8,128)(2,1)S(1)} %get-tuple-element.24.refs_0_.refs_5_, bf16[256,512]{1,0:T(8,128)(2,1)S(1)} %collective-permute-done.refs_1_, bf16[256,512]{1,0:T(8,128)(2,1)S(1)} %collective-permute-done.1.refs_2_, ...), custom_call_target="tpu_custom_call" | custom-call | tf_op jit(solution)/shard_map/pallas_call | solution.py:184
  26.6 0.7 %collective-permute-done.12.other = bf16[256,512]{1,0:T(8,128)(2,1)S(1)} collective-permute-done((bf16[256,512]{1,0:T(8,128)(2,1)S(1)}, bf16[256,512]{1,0:T(8,128)(2,1)S(1)}, u32[]{:S(2)}, u32[]{:S(2)}) %collective-permute-start.12) | collective-permute-done | bytes 262176 | tf_op jit(solution)/shard_map/ppermute | solution.py:17
  27.3 0.3 shard_map.41
  27.6 0.2 collective-permute-start.13
  27.8 1.0 %collective-permute-done.13 = f32[1,512]{1,0:T(1,128)S(1)} collective-permute-done((f32[1,512]{1,0:T(1,128)S(1)}, f32[1,512]{1,0:T(1,128)S(1)}, u32[]{:S(2)}, u32[]{:S(2)}) %collective-permute-start.13) | collective-permute-done | bytes 2080 | tf_op jit(solution)/shard_map/ppermute | solution.py:17
  28.8 0.4 %collective-permute-start.14 = (f32[1,512]{1,0:T(1,128)S(1)}, f32[1,512]{1,0:T(1,128)S(1)}, u32[]{:S(2)}, u32[]{:S(2)}) collective-permute-start(f32[1,512]{1,0:T(1,128)S(1)} %add.9), channel_id=1, source_target_pairs={{0,8},{4,12},{8,0},{12,4},{16,24},{20,28},{24,16},{28,20},{1,9},{5... | collective-permute-start | bytes 6152 | tf_op jit(solution)/shard_map/ppermute | solution.py:17
  29.2 3.2 %collective-permute-done.14 = f32[1,512]{1,0:T(1,128)S(1)} collective-permute-done((f32[1,512]{1,0:T(1,128)S(1)}, f32[1,512]{1,0:T(1,128)S(1)}, u32[]{:S(2)}, u32[]{:S(2)}) %collective-permute-start.14) | collective-permute-done | bytes 2080 | tf_op jit(solution)/shard_map/ppermute | solution.py:17
  32.4 3.2 %collective-permute-start.15 = (f32[1,512]{1,0:T(1,128)S(1)}, f32[1,512]{1,0:T(1,128)S(1)}, u32[]{:S(2)}, u32[]{:S(2)}) collective-permute-start(f32[1,512]{1,0:T(1,128)S(1)} %add.10), channel_id=1, source_target_pairs={{0,16},{4,20},{8,24},{12,28},{16,0},{20,4},{24,8},{28,12},{1,17},{... | collective-permute-start | bytes 6152 | tf_op jit(solution)/shard_map/ppermute | solution.py:17
  35.6 1.6 %collective-permute-done.15 = f32[1,512]{1,0:T(1,128)S(1)} collective-permute-done((f32[1,512]{1,0:T(1,128)S(1)}, f32[1,512]{1,0:T(1,128)S(1)}, u32[]{:S(2)}, u32[]{:S(2)}) %collective-permute-start.15) | collective-permute-done | bytes 2080 | tf_op jit(solution)/shard_map/ppermute | solution.py:17
  37.2 0.9 %broadcast_multiply_fusion = f32[256,512]{1,0:T(8,128)} fusion(f32[256,512]{1,0:T(8,128)S(1)} %get-tuple-element.25, f32[512]{0:T(512)S(1)} %bitcast.1), kind=kLoop, calls=%fused_computation | loop fusion | flops 131072 | bytes 1050624 | tf_op jit(solution)/shard_map/mul | solution.py:211
  (5 shorter events, 0.1 us)
Async XLA Ops:
  1.0 9.3 %collective-permute-start.1 = (bf16[256,512]{1,0:T(8,128)(2,1)S(1)}, bf16[256,512]{1,0:T(8,128)(2,1)S(1)}, u32[]{:S(2)}, u32[]{:S(2)}) collective-permute-start(bf16[256,512]{1,0:T(8,128)(2,1)S(1)} %get-tuple-element.24.refs_0_.refs_5_), channel_id=1, source_target_pairs={{0,2},{1,3},{2,0},{3,1},{4,6},{5,7},{6,4},{7,5},{8,10},{9,11},{10,... | collective-permute-start | bytes 786440 | tf_op jit(solution)/shard_map/ppermute | solution.py:17
  4.1 10.9 %collective-permute-start = (bf16[256,512]{1,0:T(8,128)(2,1)S(1)}, bf16[256,512]{1,0:T(8,128)(2,1)S(1)}, u32[]{:S(2)}, u32[]{:S(2)}) collective-permute-start(bf16[256,512]{1,0:T(8,128)(2,1)S(1)} %get-tuple-element.24.refs_0_.refs_5_), channel_id=1, source_target_pairs={{0,1},{1,0},{2,3},{3,2},{4,5},{5,4},{6,7},{7,6},{8,9},{9,8},{10,11... | collective-permute-start | bytes 786440 | tf_op jit(solution)/shard_map/ppermute | solution.py:17
  5.5 9.4 %collective-permute-start.3 = (bf16[128,512]{1,0:T(8,128)(2,1)S(1)}, bf16[128,512]{1,0:T(8,128)(2,1)S(1)}, u32[]{:S(2)}, u32[]{:S(2)}) collective-permute-start(bf16[128,512]{1,0:T(8,128)(2,1)S(1)} %get-tuple-element.18), channel_id=1, source_target_pairs={{0,16},{4,20},{8,24},{12,28},{16,0},{20,4},{24,8},{28,12},{1,17},{... | collective-permute-start | bytes 393224 | tf_op jit(solution)/shard_map/ppermute | solution.py:21
  8.1 15.5 %collective-permute-start.5 = (bf16[256,512]{1,0:T(8,128)(2,1)S(1)}, bf16[256,512]{1,0:T(8,128)(2,1)S(1)}, u32[]{:S(2)}, u32[]{:S(2)}) collective-permute-start(bf16[256,512]{1,0:T(8,128)(2,1)S(1)} %get-tuple-element.24.refs_0_.refs_5_), channel_id=1, source_target_pairs={{0,8},{4,12},{8,0},{12,4},{16,24},{20,28},{24,16},{28,20},{1,9},{5... | collective-permute-start | bytes 786440 | tf_op jit(solution)/shard_map/ppermute | solution.py:21
  9.7 9.1 %collective-permute-start.4 = (bf16[128,512]{1,0:T(8,128)(2,1)S(1)}, bf16[128,512]{1,0:T(8,128)(2,1)S(1)}, u32[]{:S(2)}, u32[]{:S(2)}) collective-permute-start(bf16[128,512]{1,0:T(8,128)(2,1)S(1)} %get-tuple-element.19), channel_id=1, source_target_pairs={{0,16},{4,20},{8,24},{12,28},{16,0},{20,4},{24,8},{28,12},{1,17},{... | collective-permute-start | bytes 393224 | tf_op jit(solution)/shard_map/ppermute | solution.py:21
  10.4 13.8 %collective-permute-start.2 = (bf16[256,512]{1,0:T(8,128)(2,1)S(1)}, bf16[256,512]{1,0:T(8,128)(2,1)S(1)}, u32[]{:S(2)}, u32[]{:S(2)}) collective-permute-start(bf16[256,512]{1,0:T(8,128)(2,1)S(1)} %collective-permute-done.1.refs_2_), channel_id=1, source_target_pairs={{0,1},{1,0},{2,3},{3,2},{4,5},{5,4},{6,7},{7,6},{8,9},{9,8},{10,11... | collective-permute-start | bytes 786440 | tf_op jit(solution)/shard_map/ppermute | solution.py:17
  14.9 10.7 %collective-permute-start.11 = (bf16[256,512]{1,0:T(8,128)(2,1)S(1)}, bf16[256,512]{1,0:T(8,128)(2,1)S(1)}, u32[]{:S(2)}, u32[]{:S(2)}) collective-permute-start(bf16[256,512]{1,0:T(8,128)(2,1)S(1)} %get-tuple-element.24.refs_0_.refs_5_), channel_id=1, source_target_pairs={{8,16},{12,20},{16,8},{20,12},{9,17},{13,21},{17,9},{21,13},{10,18... | collective-permute-start | bytes 786440 | tf_op jit(solution)/shard_map/ppermute | solution.py:21
  15.6 8.0 %collective-permute-start.8 = (bf16[128,512]{1,0:T(8,128)(2,1)S(1)}, bf16[128,512]{1,0:T(8,128)(2,1)S(1)}, u32[]{:S(2)}, u32[]{:S(2)}) collective-permute-start(bf16[128,512]{1,0:T(8,128)(2,1)S(1)} %collective-permute-done.3.top), channel_id=1, source_target_pairs={{8,0},{12,4},{16,24},{20,28},{9,1},{13,5},{17,25},{21,29},{10,2},{... | collective-permute-start | bytes 393224 | tf_op jit(solution)/shard_map/ppermute | solution.py:21
  18.8 6.8 %collective-permute-start.10 = (bf16[128,512]{1,0:T(8,128)(2,1)S(1)}, bf16[128,512]{1,0:T(8,128)(2,1)S(1)}, u32[]{:S(2)}, u32[]{:S(2)}) collective-permute-start(bf16[128,512]{1,0:T(8,128)(2,1)S(1)} %collective-permute-done.4.bottom), channel_id=1, source_target_pairs={{8,0},{12,4},{16,24},{20,28},{9,1},{13,5},{17,25},{21,29},{10,2},{... | collective-permute-start | bytes 393224 | tf_op jit(solution)/shard_map/ppermute | solution.py:21
  23.7 2.1 %collective-permute-start.6 = (bf16[256,512]{1,0:T(8,128)(2,1)S(1)}, bf16[256,512]{1,0:T(8,128)(2,1)S(1)}, u32[]{:S(2)}, u32[]{:S(2)}) collective-permute-start(bf16[256,512]{1,0:T(8,128)(2,1)S(1)} %shard_map.38.refs_4_), channel_id=1, source_target_pairs={{0,4},{4,0},{8,12},{12,8},{16,20},{20,16},{24,28},{28,24},{1,5},{5... | collective-permute-start | bytes 786440 | tf_op jit(solution)/shard_map/ppermute | solution.py:17
  23.7 2.1 %collective-permute-start.9 = (bf16[256,512]{1,0:T(8,128)(2,1)S(1)}, bf16[256,512]{1,0:T(8,128)(2,1)S(1)}, u32[]{:S(2)}, u32[]{:S(2)}) collective-permute-start(bf16[256,512]{1,0:T(8,128)(2,1)S(1)} %collective-permute-done.5.refs_6_), channel_id=1, source_target_pairs={{0,4},{4,0},{8,12},{12,8},{16,20},{20,16},{24,28},{28,24},{1,5},{5... | collective-permute-start | bytes 786440 | tf_op jit(solution)/shard_map/ppermute | solution.py:17
  24.2 1.8 %collective-permute-start.7 = (bf16[256,512]{1,0:T(8,128)(2,1)S(1)}, bf16[256,512]{1,0:T(8,128)(2,1)S(1)}, u32[]{:S(2)}, u32[]{:S(2)}) collective-permute-start(bf16[256,512]{1,0:T(8,128)(2,1)S(1)} %get-tuple-element.24.refs_0_.refs_5_), channel_id=1, source_target_pairs={{0,4},{4,0},{8,12},{12,8},{16,20},{20,16},{24,28},{28,24},{1,5},{5... | collective-permute-start | bytes 786440 | tf_op jit(solution)/shard_map/ppermute | solution.py:17
  25.7 1.6 %collective-permute-start.12 = (bf16[256,512]{1,0:T(8,128)(2,1)S(1)}, bf16[256,512]{1,0:T(8,128)(2,1)S(1)}, u32[]{:S(2)}, u32[]{:S(2)}) collective-permute-start(bf16[256,512]{1,0:T(8,128)(2,1)S(1)} %shard_map.40.own), channel_id=1, source_target_pairs={{0,4},{4,0},{8,12},{12,8},{16,20},{20,16},{24,28},{28,24},{1,5},{5... | collective-permute-start | bytes 786440 | tf_op jit(solution)/shard_map/ppermute | solution.py:17
  27.6 1.2 %collective-permute-start.13 = (f32[1,512]{1,0:T(1,128)S(1)}, f32[1,512]{1,0:T(1,128)S(1)}, u32[]{:S(2)}, u32[]{:S(2)}) collective-permute-start(f32[1,512]{1,0:T(1,128)S(1)} %get-tuple-element.26), channel_id=1, source_target_pairs={{0,4},{4,0},{8,12},{12,8},{16,20},{20,16},{24,28},{28,24},{1,5},{5... | collective-permute-start | bytes 6152 | tf_op jit(solution)/shard_map/ppermute | solution.py:17
  28.8 3.6 %collective-permute-start.14 = (f32[1,512]{1,0:T(1,128)S(1)}, f32[1,512]{1,0:T(1,128)S(1)}, u32[]{:S(2)}, u32[]{:S(2)}) collective-permute-start(f32[1,512]{1,0:T(1,128)S(1)} %add.9), channel_id=1, source_target_pairs={{0,8},{4,12},{8,0},{12,4},{16,24},{20,28},{24,16},{28,20},{1,9},{5... | collective-permute-start | bytes 6152 | tf_op jit(solution)/shard_map/ppermute | solution.py:17
  32.4 4.8 %collective-permute-start.15 = (f32[1,512]{1,0:T(1,128)S(1)}, f32[1,512]{1,0:T(1,128)S(1)}, u32[]{:S(2)}, u32[]{:S(2)}) collective-permute-start(f32[1,512]{1,0:T(1,128)S(1)} %add.10), channel_id=1, source_target_pairs={{0,16},{4,20},{8,24},{12,28},{16,0},{20,4},{24,8},{28,12},{1,17},{... | collective-permute-start | bytes 6152 | tf_op jit(solution)/shard_map/ppermute | solution.py:17
